TPU v7x, 256 devices: a whole 4x4x8 slice. The times are simulated.
256 devices in a mesh: tok: 32 (over y, z), head: 8 (over x, core).
Axes of the slice: x: 4, y: 4, z: 8, core: 2. Of those that a mesh axis runs over, the one named last changes fastest.
Arguments:
- guess: float32 [4096, 1024], P('tok', 'head'), may hold values from -4 to 4
- drive: float32 [4096, 1024], P('tok', 'head'), may hold values from -2 to 2
- decay: float32 [4096, 1024], P('tok', 'head'), may hold values from 0 to 1
- mixing: float32 [1024], P('head'), may hold values from 0.1 to 0.5
- init_state: float32 [1024], P('head'), may hold values from -6 to 6
- skew_gen: float32 [8, 128, 128], P('head'), as said below
- w_up: bfloat16 [1024, 4096], P(None, 'head'), may hold values from -0.1875 to 0.1875
- w_down: bfloat16 [1024, 4096], P(None, 'head'), may hold values from -0.09375 to 0.09375
- cotangent: bfloat16 [4096, 1024], P('tok', 'head'), may hold values from -6 to 6
Outputs:
- states: float32 [4096, 1024], P('tok', 'head')
- mlp_out: bfloat16 [4096, 1024], P('tok', 'head')
- state_grad: bfloat16 [4096, 1024], P('tok', 'head')
- grad_up: float32 [1024, 4096], P('tok', 'head')
- grad_down: float32 [1024, 4096], P('tok', 'head')
Inputs may be any that keep to these rules, and one draw needn't show every extreme that they name: `skew_gen`: each head's matrix is skew-symmetric.
All inputs are finite; a program needn't handle non-finite values.
Results may differ from a plain program's by a relative error of at most 0.017.
Values may be sent and summed in bfloat16 or wider, within the bound.
A program may use at most 64 MiB of HBM per device.

v0:
```python
import jax
import jax.numpy as jnp
from jax import lax
from jax.sharding import PartitionSpec as P

BLK = 32


exact_precision = lax.Precision.HIGHEST


def from_behind(block, axis, distance):
    devices = range(lax.axis_size(axis))
    route = [(i - distance, i) for i in devices if i - distance in devices]
    return lax.ppermute(block, axis, route)


def prefix(value, axis, join, neutral):
    count, mine = (lax.axis_size(axis), lax.axis_index(axis))
    pieces = jax.tree.map(lambda part: lax.all_gather(part, axis), value)
    running = jax.tree.map(
        lambda part, zero: jnp.full_like(part, 0) + jnp.asarray(zero, part.dtype), value, neutral
    )

    def lap(position, running):
        longer = join(running, jax.tree.map(lambda part: part[position], pieces))
        return jax.tree.map(lambda new, old: jnp.where(position < mine, new, old), longer, running)

    return lax.fori_loop(0, count - 1, lap, running)


def cayley(antisymmetric_matrix):
    identity = jnp.eye(antisymmetric_matrix.shape[0], dtype=jnp.float32)
    raised = identity + antisymmetric_matrix
    shifted = identity - jnp.dot(
        antisymmetric_matrix, antisymmetric_matrix, precision=exact_precision
    )
    factor = jnp.linalg.cholesky(shifted)
    squared = jnp.dot(raised, raised, precision=exact_precision)
    return jax.scipy.linalg.cho_solve((factor, True), squared.T).T


def tangent_approximate(before, decay, mixing):
    bent_values = jnp.tanh(before)
    curvature = 1.0 - bent_values * bent_values
    gradient_inclines = (1.0 - mixing) * decay + mixing * curvature
    pushes = mixing * (bent_values - curvature * before)
    return (gradient_inclines, pushes)


def combine_couple(earlier, later):
    joined_map = jnp.dot(later[0], earlier[0], precision=exact_precision)
    joined_shift = jnp.dot(later[0], earlier[1], precision=exact_precision) + later[1]
    return (joined_map, joined_shift)


def tree_top(jacobians, offsets):
    level_maps, shifts = (jacobians, offsets)
    while level_maps.shape[0] > 1:
        later_maps = level_maps[1::2]
        joined = jnp.einsum("bij,bjk->bik", later_maps, level_maps[0::2], precision=exact_precision)
        moved_shifts = (
            jnp.einsum("bij,bj->bi", later_maps, shifts[0::2], precision=exact_precision)
            + shifts[1::2]
        )
        level_maps, shifts = (joined, moved_shifts)
    return (level_maps[0], shifts[0])


def on_device(guess, drive, decay, mixing, init_state, skew_gen, w_up, w_down, cotangent):
    tok_rows, state_width = guess.shape
    rotation = cayley(skew_gen[0])
    received = from_behind(guess[tok_rows - 1 :], "tok", 1)
    leading = lax.axis_index("tok") == 0
    previous = jnp.where(leading, init_state[None, :], received)
    before = jnp.concatenate([previous, guess[:-1]], axis=0)
    gradient_inclines, pushes = tangent_approximate(before, decay, mixing[None, :])
    offsets = jnp.dot(pushes, rotation.T, precision=exact_precision) + drive
    block_count = tok_rows // BLK
    slope_blocks = gradient_inclines.reshape(block_count, BLK, state_width)
    offset_blocks = offsets.reshape(block_count, BLK, state_width)
    identity = jnp.eye(state_width, dtype=jnp.float32)
    zero_shift = jnp.zeros((state_width,), jnp.float32)

    def summarize(carried, inputs):
        slope_block, offset_block = inputs
        block_map = tree_top(rotation[None, :, :] * slope_block[:, None, :], offset_block)
        return (combine_couple(carried, block_map), block_map)

    group_map, block_maps = lax.scan(
        summarize, (identity, zero_shift), (slope_blocks, offset_blocks)
    )
    prefix_map, prefix_shift = prefix(
        (group_map[0], group_map[1]), "tok", combine_couple, (identity, zero_shift)
    )
    entering = jnp.dot(prefix_map, init_state, precision=exact_precision) + prefix_shift

    def advance_block(carried, block_map):
        return (jnp.dot(block_map[0], carried, precision=exact_precision) + block_map[1], carried)

    final_state, block_entries = lax.scan(advance_block, entering, block_maps)
    slope_steps = jnp.swapaxes(slope_blocks, 0, 1)
    offset_steps = jnp.swapaxes(offset_blocks, 0, 1)

    def step_one_token(carried, inputs):
        slope_row, bias_vector_line = inputs
        following = (
            jnp.dot(slope_row * carried, rotation.T, precision=exact_precision) + bias_vector_line
        )
        return (following, following)

    last_rows, state_steps = lax.scan(step_one_token, block_entries, (slope_steps, offset_steps))
    states = jnp.swapaxes(state_steps, 0, 1).reshape(tok_rows, state_width)
    features = lax.all_gather(states.astype(jnp.bfloat16), "head", axis=1, tiled=True)
    hidden_pre = jnp.dot(features, w_up, preferred_element_type=jnp.float32)
    logistic_gate = jax.nn.sigmoid(hidden_pre)
    hidden = (hidden_pre * logistic_gate).astype(jnp.bfloat16)
    out_terms = lax.dot_general(
        hidden, w_down, (((1,), (1,)), ((), ())), preferred_element_type=jnp.float32
    )
    mlp_out = lax.psum_scatter(
        out_terms.astype(jnp.bfloat16), "head", scatter_dimension=1, tiled=True
    )
    cot_whole = lax.all_gather(cotangent, "head", axis=1, tiled=True)
    hidden_grad = jnp.dot(cot_whole, w_down, preferred_element_type=jnp.float32)
    pre_grad = (hidden_grad * logistic_gate * (1.0 + hidden_pre * (1.0 - logistic_gate))).astype(
        jnp.bfloat16
    )
    state_terms = lax.dot_general(
        pre_grad, w_up, (((1,), (1,)), ((), ())), preferred_element_type=jnp.float32
    )
    state_grad = lax.psum_scatter(
        state_terms.astype(jnp.bfloat16), "head", scatter_dimension=1, tiled=True
    )
    up_terms = lax.dot_general(
        features, pre_grad, (((0,), (0,)), ((), ())), preferred_element_type=jnp.float32
    )
    down_terms = lax.dot_general(
        cot_whole, hidden, (((0,), (0,)), ((), ())), preferred_element_type=jnp.float32
    )
    total_up, total_down = (
        lax.psum(up_terms.astype(jnp.bfloat16), "tok").astype(jnp.float32),
        lax.psum(down_terms.astype(jnp.bfloat16), "tok").astype(jnp.float32),
    )
    share_rows = total_up.shape[0] // lax.axis_size("tok")
    first_row = lax.axis_index("tok") * share_rows
    grad_up = lax.dynamic_slice_in_dim(total_up, first_row, share_rows, 0)
    grad_down = lax.dynamic_slice_in_dim(total_down, first_row, share_rows, 0)
    return (states, mlp_out, state_grad, grad_up, grad_down)


def solution(mesh):
    placed = (
        P("tok", "head"),
        P("tok", "head"),
        P("tok", "head"),
        P("head"),
        P("head"),
        P("head", None, None),
        P(None, "head"),
        P(None, "head"),
        P("tok", "head"),
    )
    return jax.shard_map(
        on_device,
        mesh=mesh,
        in_specs=placed,
        out_specs=(
            P("tok", "head"),
            P("tok", "head"),
            P("tok", "head"),
            P("tok", "head"),
            P("tok", "head"),
        ),
        check_vma=False,
    )
```

profile of v0, /device:TPU:8, one launch (start us, length us, event | category | flops | bytes accessed | tf_op | source)
XLA Modules:
  0.0 470.9 jit_solution(7339539034221796910)
XLA Ops:
  8.0 3.8 collective-permute-start
  11.9 1.1 fusion.58
  13.0 1.2 fusion.50
  15.0 11.7 %cholesky.14 = f32[128,128]{1,0:T(8,128)S(1)} custom-call(f32[128,128]{1,0:T(8,128)S(1)} %fusion.57), custom_call_target="Cholesky" | custom-call | tf_op jit(solution)/shard_map/jit(cholesky)/cholesky | solution.py:38
  28.0 9.8 %custom-call.10 = f32[1,128,128]{1,2,0:T(8,128)S(1)} custom-call(f32[1,128,128]{2,1,0:T(8,128)S(1)} %fusion.49), custom_call_target="InvertDiagBlocksLowerTriangular" | custom-call | tf_op jit(solution)/shard_map/jit(_cho_solve)/triangular_solve | solution.py:40
  39.1 1.1 convolution_add_fusion.2
  41.2 29.6 %while.59 = (s32[]{:T(128)}, f32[128,128]{1,0:T(8,128)S(1)}, f32[128]{0:T(128)S(1)}, f32[4,128,128]{2,1,0:T(8,128)S(1)}, f32[4,128]{1,0:T(4,128)S(1)}, /*index=5...) while((s32[]{:T(128)}, f32[128,128]{1,0:T(8,128)S(1)}, ...), condition=%wide.region_3.4_spmd.clone, body=%wide.region_2.3_spmd.clone.sunk | while | flops 812126336 | bytes 10973315 | solution.py:90
  41.5 1.7 fusion.167
  43.2 1.2 fusion.162
  48.9 1.7 fusion.167
  50.6 1.2 fusion.162
  56.3 1.7 fusion.167
  58.0 1.2 fusion.162
  63.7 1.7 fusion.167
  65.4 1.2 fusion.162
  71.7 12.2 %all_gather.23 = bf16[128,1024]{1,0:T(8,128)(2,1)S(1)} all-gather(bf16[128,128]{1,0:T(8,128)(2,1)S(1)} %copy-done.3), channel_id=1, replica_groups=mesh['tok'=32,'head'=8] {'head'}, dimensions={1}, use_global_device_ids=true | all-gather | bytes 294912 | tf_op jit(solution)/shard_map/all_gather | solution.py:124
  83.9 40.9 %all-gather.2 = f32[32,1,128]{2,1,0:T(1,128)S(1)} all-gather(f32[1,1,128]{2,1,0:T(1,128)S(1)} %bitcast.263), channel_id=3, replica_groups=mesh['tok'=32,'head'=8] {'tok'}, dimensions={0}, use_global_device_ids=true | all-gather | bytes 16896 | tf_op jit(solution)/shard_map/all_gather | solution.py:20
  124.8 25.4 %all-gather.5.cloned.1.call-done = f32[4096,128]{1,0:T(8,128)} async-done(((f32[128,128]{1,0:T(8,128)}), f32[4096,128]{1,0:T(8,128)}) %all-gather.5.cloned.1.call-update) | async-done | bytes 2097168 | tf_op jit(solution)/shard_map/all_gather | solution.py:20
  150.2 67.2 %while.60 = (s32[]{:T(128)}, f32[128,128]{1,0:T(8,128)S(1)}, f32[128]{0:T(128)S(1)}, s32[]{:T(128)}, f32[32,128,128]{2,1,0:T(8,128)}, /*index=5*/f32[32,128]{1,0:T(8,128)S(1)}, s32[]{:T(128)}, s32[]{:T(128)}) while((s32[]{:T(128)}, f32[128,128]{1,0:T(8,128)S(1)}, f32[128]{0:T(128)S(1)}, s32[]{:T(128)}, f32[32,128,128]{2,1,0:T(8,128)}, ...), condition=%wide.region_5.6_spmd.clone, body=%wide.region_4.5_spmd.clone.sunk | while | flops 25379332 | bytes 464500 | solution.py:29
  151.3 1.1 convolution_select_fusion.2
  153.4 1.1 convolution_select_fusion.2
  155.6 1.1 convolution_select_fusion.2
  157.8 1.1 convolution_select_fusion.2
  159.9 1.1 convolution_select_fusion.2
  161.1 1.0 fusion.176
  162.1 1.1 convolution_select_fusion.2
  163.3 1.0 fusion.176
  164.3 1.1 convolution_select_fusion.2
  165.4 1.0 fusion.176
  166.4 1.1 convolution_select_fusion.2
  168.6 1.1 convolution_select_fusion.2
  170.8 1.1 convolution_select_fusion.2
  173.0 1.1 convolution_select_fusion.2
  175.1 1.1 convolution_select_fusion.2
  177.3 1.1 convolution_select_fusion.2
  179.5 1.1 convolution_select_fusion.2
  181.6 1.1 convolution_select_fusion.2
  183.8 1.1 convolution_select_fusion.2
  186.0 1.1 convolution_select_fusion.2
  188.1 1.1 convolution_select_fusion.2
  190.3 1.1 convolution_select_fusion.2
  192.5 1.1 convolution_select_fusion.2
  194.7 1.1 convolution_select_fusion.2
  196.8 1.1 convolution_select_fusion.2
  199.0 1.1 convolution_select_fusion.2
  201.2 1.1 convolution_select_fusion.2
  203.3 1.1 convolution_select_fusion.2
  205.5 1.1 convolution_select_fusion.2
  207.7 1.1 convolution_select_fusion.2
  209.8 1.1 convolution_select_fusion.2
  212.0 1.1 convolution_select_fusion.2
  214.2 1.1 convolution_select_fusion.2
  216.3 1.1 convolution_select_fusion.2
  217.7 1.1 while.57
  218.7 6.4 %while.58 = (s32[]{:T(128)}, f32[4,128]{1,0:T(4,128)S(1)}, f32[32,4,128]{2,1,0:T(4,128)S(1)}, f32[32,4,128]{2,0,1:T(8,128)S(1)}, f32[128,128]{1,0:T(8,128)S(1)}, /*index=5*/f32[32,4,128]{2,0,1:T(8,128)S(1)}, s32[]{:T(128)}) while((s32[]{:T(128)}, f32[4,128]{1,0:T(4,128)S(1)}, f32[32,4,128]{2,1,0:T(4,128)S(1)}, f32[32,4,128]{2,0,1:T(8,128)S(1)}, ...), condition=%wide.region_9.10_spmd, body=%wide.region_8.9_spmd.sunk | while | flops 787458 | bytes 88157 | solution.py:112
  225.2 12.2 %all_gather.22 = bf16[128,1024]{1,0:T(8,128)(2,1)S(1)} all-gather(bf16[128,128]{1,0:T(8,128)(2,1)S(1)} %bitcast_convert_fusion), channel_id=1, replica_groups=mesh['tok'=32,'head'=8] {'head'}, dimensions={1}, use_global_device_ids=true | all-gather | bytes 294912 | tf_op jit(solution)/shard_map/all_gather | solution.py:114
  240.9 1.4 convolution_convert_fusion.1
  242.3 1.5 fusion.45
  243.8 26.8 %reduce-scatter.9.cloned.1.call-done = bf16[128,128]{1,0:T(8,128)(2,1)} async-done(((bf16[1024,128]{1,0:T(8,128)(2,1)}), bf16[128,128]{1,0:T(8,128)(2,1)}) %reduce-scatter.9.cloned.1.call-update) | async-done | bytes 32784
  270.5 1.5 copy.37
  272.0 33.4 %reduce-scatter.7.cloned.1.call-done = bf16[128,128]{1,0:T(8,128)(2,1)} async-done(((bf16[1024,128]{1,0:T(8,128)(2,1)}), bf16[128,128]{1,0:T(8,128)(2,1)}) %reduce-scatter.7.cloned.1.call-update) | async-done | bytes 32784
  305.4 1.5 copy.35
  306.8 154.4 %all-reduce.3.cloned.1.call-done = (bf16[1024,512]{1,0:T(8,128)(2,1)}, bf16[1024,512]{0,1:T(8,128)(2,1)}) async-done(((bf16[1024,512]{1,0:T(8,128)(2,1)}, bf16[1024,512]{0,1:T(8,128)(2,1)}), (bf16[1024,512]{1,0:T(8,128)(2,1)}, bf16[1024,512]{0,1:T(8,128)(2,1)})) %all-reduce.3.cloned.1.call-update) | async-done | bytes 2097168 | tf_op jit(solution)/shard_map/psum | solution.py:142
  461.2 1.4 dynamic-slice_convert_fusion.1
  (358 shorter events, 64.9 us)
Async XLA Ops:
  7.2 230.2 %copy-start = (bf16[1024,512]{1,0:T(8,128)(2,1)S(1)}, bf16[1024,512]{1,0:T(8,128)(2,1)}, u32[]{:S(2)}) copy-start(bf16[1024,512]{1,0:T(8,128)(2,1)} %param.23) | copy-start | bytes 3145732
  7.2 143.0 %all-gather.5.cloned.1.call-start = ((), (), s32[]{:S(2)}) async-start(), calls=%async_computation.2 | async-start | bytes 2162688 | tf_op jit(solution)/shard_map/all_gather | solution.py:20
  8.0 30.5 %collective-permute-start = (f32[1,128]{1,0:T(1,128)S(1)}, f32[1,128]{1,0:T(1,128)S(1)}, u32[]{:S(2)}, u32[]{:S(2)}) collective-permute-start(f32[1,128]{1,0:T(1,128)S(1)} %slice.88), channel_id=1, source_target_pairs={{0,8},{8,16},{16,24},{24,32},{32,40},{40,48},{48,56},{56,64},{64,7... | collective-permute-start | bytes 1544 | tf_op jit(solution)/shard_map/ppermute | solution.py:15
  41.2 30.5 %copy-start.3 = (bf16[128,128]{1,0:T(8,128)(2,1)S(1)}, bf16[128,128]{1,0:T(8,128)(2,1)}, u32[]{:S(2)}) copy-start(bf16[128,128]{1,0:T(8,128)(2,1)} %param.25) | copy-start | bytes 98308
  70.8 0.6 copy-start.1
  70.8 146.7 %copy-start.4 = (f32[128]{0:T(128)S(1)}, f32[128]{0:T(128)}, u32[]{:S(2)}) copy-start(f32[128]{0:T(128)} %param.21) | copy-start | bytes 1540
  71.4 199.1 %reduce-scatter.9.cloned.1.call-start = ((), (), s32[]{:S(2)}) async-start(), calls=%async_computation.4 | async-start | bytes 294912
  217.5 20.2 %copy-start.5 = (bf16[1024,512]{1,0:T(8,128)(2,1)S(1)}, bf16[1024,512]{1,0:T(8,128)(2,1)}, u32[]{:S(2)}) copy-start(bf16[1024,512]{1,0:T(8,128)(2,1)} %param.24) | copy-start | bytes 3145732
  225.2 12.9 %copy-start.2 = (f32[4,32,128]{2,1,0:T(8,128)}, f32[4,32,128]{2,1,0:T(8,128)S(1)}, u32[]{:S(2)}) copy-start(f32[4,32,128]{2,1,0:T(8,128)S(1)} %copy.24) | copy-start | bytes 196612
  239.4 66.0 %reduce-scatter.7.cloned.1.call-start = ((), (), s32[]{:S(2)}) async-start(), calls=%async_computation.3 | async-start | bytes 294912
  240.8 220.4 %all-reduce.3.cloned.1.call-start = ((), (), s32[]{:S(2)}) async-start(), calls=%async_computation.5 | async-start | bytes 4194304 | tf_op jit(solution)/shard_map/psum | solution.py:142
Sparse Core Ops, SparseCore 0:
  71.5 78.6 all-gather.4
  239.5 30.9 reduce-scatter.8
  273.1 32.2 reduce-scatter.6
  308.9 152.2 all-reduce.2
where the time goes:
time: 476 us; the launch traced here: 471 us
  waiting for transfers between devices  240 us (50%)
  matrix products  107 us (22%)
  blocking collectives  65.3 us (14%)
  other arithmetic  28.5 us (6%)
  between operations  14.1 us (3%)
  local copies, waits for them, and re-layouts  9.27 us (2%)
    psum x1, waiting for transfers between devices, on_device(): lax.psum(up_terms.astype(jnp.bfloat16), 'tok').astype(jnp.float32)  154 us
    unnamed x6, waiting for transfers between devices  60.2 us
    all_gather x1, blocking collectives, prefix(): pieces = jax.tree.map(lambda part: lax.all_gather(part, axis), value)  40.9 us
    dot_general x35, matrix products, combine_couple(): joined_map = jnp.dot(later[0], earlier[0], precision=exact_precision)  34.8 us
    dot_general x35, matrix products, combine_couple(): jnp.dot(later[0], earlier[1], precision=exact_precision) + later[1]  32.5 us
    all_gather x1, waiting for transfers between devices, prefix(): pieces = jax.tree.map(lambda part: lax.all_gather(part, axis), value)  25.4 us
    dot_general x20, matrix products, tree_top(): jnp.einsum('bij,bj->bi', later_maps, shifts[0::2], precision=exact_precis...  14.5 us
    another operation x3, other arithmetic, cayley(): factor = jnp.linalg.cholesky(shifted)  12.4 us
  transfers between devices with their start and end apart: 5, of which 4 were waited for; matrix products, arithmetic and copies ran while one was open for 7% of the time, Pallas kernels for 0%

commit v1 on v0

v1 whole, which is shorter than its diff:
```python
import functools

import jax
import jax.numpy as jnp
from jax import lax
from jax.experimental import pallas as pl
from jax.experimental.pallas import tpu as pltpu
from jax.sharding import PartitionSpec as P

MESH = pl.DeviceIdType.MESH
F32, BF16 = jnp.float32, jnp.bfloat16
S = 128
NZ = 8
NB, L = 8, 16
MR = 144
SENT = 136
CUT = 72
NEWTON = 14


def split(x):
    hi = x.astype(BF16)
    return hi, (x - hi.astype(F32)).astype(BF16)


def left(x):
    return jnp.concatenate(split(x), axis=1)


def right(x):
    both = jnp.concatenate(split(x), axis=1)
    return jnp.concatenate([both, both], axis=0)


def product(l, r):
    out = jnp.dot(l, r, preferred_element_type=F32)
    return out[:, :S] + out[:, S:]


def mm(a, b):
    return product(left(a), right(b))


def compose(first, then):
    out = mm(first, then[:S])
    return jnp.concatenate([out[:S], out[S:] + then[S:]], axis=0)


def eye():
    rows = lax.broadcasted_iota(jnp.int32, (S, S), 0)
    cols = lax.broadcasted_iota(jnp.int32, (S, S), 1)
    return jnp.where(rows == cols, 1.0, 0.0).astype(F32)


def column(v, unit):
    return jnp.sum(unit * v, axis=1, keepdims=True)


def apply_map(v, m, unit):
    return jnp.sum(column(v, unit) * m[:S], axis=0, keepdims=True) + m[S : S + 1]


def dot_t(a, b):
    return lax.dot_general(a, b, (((1,), (1,)), ((), ())), preferred_element_type=F32)


class Ring:
    def __init__(self, n, me, device, blocks, landing, send, recv, half):
        self.n, self.me, self.device = n, me, device
        self.blocks, self.landing, self.send, self.recv, self.half = blocks, landing, send, recv, half

    def piece(self, owner, c):
        return self.blocks.at[owner, pl.ds(c * self.half, self.half)]

    def copy(self, d, hop, c):
        way = 1 if d == 0 else -1
        owner = lax.rem(self.me + way * (self.n // 2 - hop) + 2 * self.n, self.n)
        target = lax.rem(self.me + way + self.n, self.n)
        return pltpu.make_async_remote_copy(
            src_ref=self.piece(owner, c),
            dst_ref=self.landing.at[d, hop, c],
            send_sem=self.send.at[d, hop, c],
            recv_sem=self.recv.at[d, hop, c],
            device_id=self.device(target),
            device_id_type=MESH,
        )

    def begin(self):
        for d in range(2):
            self.copy(d, 0, d).start()
        if self.n > 2:
            for d in range(2):
                self.copy(d, 1, 1 - d).start()

    def pieces(self, hop):
        return [(d, c) for c in range(2) for d in range(2) if hop > 0 or c == d]

    def advance(self, hop):
        last = hop == self.n // 2 - 1
        order = [(d, 1 - d) for d in range(2)] + [(d, d) for d in range(2)]
        for d, c in order:
            if hop == 0 and c != d:
                continue
            self.copy(d, hop, c).wait_recv()
            if last:
                continue
            way = 1 if d == 0 else -1
            owner = lax.rem(self.me + way * (self.n // 2 - hop - 1) + 2 * self.n, self.n)
            mine = self.blocks[owner, pl.ds(c * self.half, self.half)]
            came = self.landing[d, hop, c]
            if not (hop == 0 and False):
                self.blocks[owner, pl.ds(c * self.half, self.half)] = (
                    mine.astype(F32) + came.astype(F32)
                ).astype(BF16)
            self.copy(d, hop + 1, c).start()

    def total(self, c):
        last = self.n // 2 - 1
        out = self.blocks[self.me, pl.ds(c * self.half, self.half)].astype(F32)
        for d in range(2):
            if (d, c) in self.pieces(last):
                out = out + self.landing[d, last, c].astype(F32)
        return out

    def finish(self):
        for hop in range(self.n // 2):
            for d, c in self.pieces(hop):
                self.copy(d, hop, c).wait_send()


def kernel(
    ntok,
    nhead,
    guess,
    drive,
    decay,
    mixing,
    init,
    skew,
    w_up_hbm,
    w_down_hbm,
    cot,
    states_out,
    mlp_out,
    sgrad_out,
    gup_out,
    gdown_out,
    w_up,
    w_down,
    w_sem,
    shifted,
    row_send,
    row_recv,
    zinv,
    wrot,
    slopes,
    offs,
    pre_maps,
    shifts,
    bmaps,
    bpre,
    gath,
    gsend,
    grecv,
    table,
    vin,
    vout,
    v_send,
    v_recv,
    feats,
    f_send,
    f_recv,
    cots,
    c_send,
    c_recv,
    hgrad,
    ftrans,
    ctrans,
    parts,
    landed,
    o_send,
    o_recv,
    ublk,
    dblk,
    u2blk,
    d2blk,
    la1,
    la2,
    lb1,
    lb2,
    a1s,
    a1r,
    a2s,
    a2r,
    b1s,
    b1r,
    b2s,
    b2r,
):
    ny, nx = ntok // NZ, nhead // 2
    tok, head = lax.axis_index("tok"), lax.axis_index("head")
    y, z = lax.div(tok, NZ), lax.rem(tok, NZ)
    x, core = lax.div(head, 2), lax.rem(head, 2)

    def along_z(target):
        return {"tok": y * NZ + target, "head": head}

    def along_y(target):
        return {"tok": target * NZ + z, "head": head}

    def at_tok(target):
        return {"tok": target, "head": head}

    def at_head(target):
        return {"tok": tok, "head": target}

    peers = [(dx, flip) for dx in ([0, 1, nx - 1, 2] if nx >= 4 else range(nx)) for flip in (1, 0)]
    peers = [q for q in peers if q != (0, 0)]

    def peer(q):
        return lax.rem(x + q[0], nx) * 2 + lax.rem(core + q[1], 2)

    after, before_me = lax.rem(tok + 1, ntok), lax.rem(tok + ntok - 1, ntok)

    barrier = pltpu.get_barrier_semaphore()
    greet = [along_z(lax.rem(z + 1, NZ)), along_z(lax.rem(z + NZ - 1, NZ))]
    greet += [along_y(lax.rem(y + 1, ny)), along_y(lax.rem(y + ny - 1, ny))]
    greet += [at_tok(after), at_tok(before_me)]
    greet += [at_head(peer(q)) for q in peers]
    for who in greet:
        pl.semaphore_signal(barrier, inc=1, device_id=who, device_id_type=MESH)
    loads = [
        pltpu.make_async_copy(w_up_hbm, w_up, w_sem.at[0]),
        pltpu.make_async_copy(w_down_hbm, w_down, w_sem.at[1]),
    ]
    for load in loads:
        load.start()

    unit = eye()
    k = skew[...]
    a = unit + k
    kk = mm(k, k)
    bound = jnp.sqrt(jnp.sum(jnp.sum(kk * kk, axis=1, keepdims=True), axis=0, keepdims=True) * 0.5)
    top = 1.0 + 1.01 * bound
    zinv[...] = (unit - k) * (2.0 / (1.0 + top))
    gap = (top - 1.0) / (top + 1.0)
    a_left = left(a)

    def newton(_, gap):
        v = zinv[...]
        t = product(a_left, right(v))
        square = gap * gap
        zinv[...] = (2.0 * v - mm(v, t)) * (2.0 / (2.0 - square))
        return square / (2.0 - square)

    gap = lax.fori_loop(0, NEWTON // 2, newton, gap)

    pl.semaphore_wait(barrier, len(greet))
    row_copy = pltpu.make_async_remote_copy(
        src_ref=guess.at[pl.ds(S - 8, 8)],
        dst_ref=shifted.at[pl.ds(0, 8)],
        send_sem=row_send,
        recv_sem=row_recv,
        device_id=at_tok(after),
        device_id_type=MESH,
    )
    row_copy.start()

    def head_copy(q, src, dst, send, recv):
        return pltpu.make_async_remote_copy(
            src_ref=src,
            dst_ref=dst,
            send_sem=send.at[q[0] * 2 + q[1]],
            recv_sem=recv.at[q[0] * 2 + q[1]],
            device_id=at_head(peer(q)),
            device_id_type=MESH,
        )

    def back(q):
        return lax.rem(x + nx - q[0], nx) * 2 + lax.rem(core + q[1], 2)

    for q in peers:
        head_copy(q, cot, cots.at[head], c_send, c_recv).start()
    cots[head] = cot[...]

    lax.fori_loop(NEWTON // 2, NEWTON, newton, gap)
    v = zinv[...]
    t = jnp.dot(a, v, precision=lax.Precision.HIGHEST, preferred_element_type=F32)
    v = v + mm(v, unit - t)
    rot_t = 2.0 * v - unit
    wrot[...] = right(rot_t)

    shifted[pl.ds(8, S), :] = guess[...]
    row_copy.wait_recv()
    before = shifted[pl.ds(7, S), :]
    first = (lax.broadcasted_iota(jnp.int32, (S, S), 0) == 0) & (tok == 0)
    before = jnp.where(first, init[...], before)
    m = mixing[...]
    bent = jnp.tanh(before)
    curve = 1.0 - bent * bent
    slopes[...] = (1.0 - m) * decay[...] + m * curve
    offs[...] = product(left(m * (bent - curve * before)), wrot[...]) + drive[...]

    def advance(step, blocks, shift):
        rows = [left(blocks[b] * slopes[pl.ds(b * L + step, 1), :]) for b in range(NB)]
        shift = shift * slopes[pl.ds(step, NB, stride=L), :]
        rows.append(left(jnp.concatenate([shift, jnp.zeros((16 - NB, S), F32)], axis=0)))
        out = product(jnp.concatenate(rows, axis=0), wrot[...])
        for b in range(NB):
            pre_maps[b * L + step] = out[b * S : (b + 1) * S]
        shifts[step] = out[NB * S : NB * S + NB] + offs[pl.ds(step, NB, stride=L), :]

    advance(0, [unit] * NB, jnp.zeros((NB, S), F32))

    def later(step, _):
        advance(step, [pre_maps[b * L + step - 1] for b in range(NB)], shifts[step - 1])
        return 0

    lax.fori_loop(1, L, later, 0)

    pad = jnp.zeros((MR - S - 1, S), F32)

    def block_map(b):
        return jnp.concatenate([pre_maps[b * L + L - 1], shifts[L - 1, b : b + 1], pad], axis=0)

    none = jnp.concatenate([unit, jnp.zeros((MR - S, S), F32)], axis=0)
    bpre[0] = none
    bpre[1] = block_map(0)
    bpre[2] = compose(block_map(0), block_map(1))
    bmaps[0] = compose(block_map(2), block_map(3))
    bmaps[1] = compose(block_map(4), block_map(5))
    bmaps[2] = compose(block_map(6), block_map(7))
    bpre[4] = compose(bpre[2], bmaps[0])
    bmaps[3] = compose(bmaps[1], bmaps[2])
    gath[z] = compose(bpre[4], bmaps[3])

    cuts = ((0, CUT), (CUT, SENT - CUT))

    def hop(d, k, c):
        way = 1 if d == 0 else -1
        part = gath.at[lax.rem(z - way * k + 2 * NZ, NZ), pl.ds(*cuts[c])]
        return pltpu.make_async_remote_copy(
            src_ref=part,
            dst_ref=part,
            send_sem=gsend.at[d, k, c],
            recv_sem=grecv.at[d, k, c],
            device_id=along_z(lax.rem(z + way + NZ, NZ)),
            device_id_type=MESH,
        )

    def arrived(d, k, c):
        way = 1 if d == 0 else -1
        part = gath.at[lax.rem(z - way * (k + 1) + 2 * NZ, NZ), pl.ds(*cuts[c])]
        pltpu.make_async_remote_copy(
            src_ref=part,
            dst_ref=part,
            send_sem=gsend.at[d, k, c],
            recv_sem=grecv.at[d, k, c],
            device_id=along_z(lax.rem(z + way + NZ, NZ)),
            device_id_type=MESH,
        ).wait_recv()

    def goes(d, k, c):
        return k < NZ // 2 - 1 or c == d

    for c in range(2):
        for d in range(2):
            hop(d, 0, c).start()

    def relay(k):
        for c in range(2):
            for d in range(2):
                if goes(d, k, c):
                    arrived(d, k, c)
                    if k + 1 < NZ // 2 and goes(d, k + 1, c):
                        hop(d, k + 1, c).start()

    for load in loads:
        load.wait()
    own = head_copy
    for q in peers:
        head_copy(q, cot, cots.at[back(q)], c_send, c_recv).wait_recv()
    hgrad[...] = jnp.zeros_like(hgrad)
    for c in range(nx):
        hgrad[...] += jnp.dot(
            jnp.concatenate([cots[2 * c], cots[2 * c + 1]], axis=1),
            w_down[pl.ds(c * 2 * S, 2 * S), :],
            preferred_element_type=F32,
        )
    relay(0)
    for h in range(nhead):
        ctrans[pl.ds(h * S, S), :] = cots[h].astype(F32).T.astype(BF16)
    bpre[3] = compose(bpre[2], block_map(2))
    bpre[5] = compose(bpre[4], block_map(4))
    relay(1)
    bpre[6] = compose(bpre[4], bmaps[1])
    bpre[7] = compose(bpre[6], block_map(6))
    gath[NZ] = none
    table[0] = none
    relay(2)
    relay(3)
    pairs = [compose(gath[2 * i], gath[2 * i + 1]) for i in range(4)]
    table[1] = pairs[0]
    table[2] = pairs[2]
    low = compose(pairs[0], pairs[1])
    table[3] = low
    whole = compose(low, compose(pairs[2], pairs[3]))

    chain = pltpu.make_async_remote_copy(
        src_ref=vout,
        dst_ref=vin,
        send_sem=v_send,
        recv_sem=v_recv,
        device_id=along_y(lax.rem(y + 1, ny)),
        device_id_type=MESH,
    )

    @pl.when(y == 0)
    def _():
        vin[...] = jnp.broadcast_to(init[...], (8, S))

    @pl.when(y > 0)
    def _():
        chain.wait_recv()

    v = vin[0:1, :]

    @pl.when(y < ny - 1)
    def _():
        vout[...] = jnp.broadcast_to(apply_map(v, whole, unit), (8, S))
        chain.start()

    za, zb, zc = lax.div(z, 4), lax.rem(lax.div(z, 2), 2), lax.rem(z, 2)
    v = apply_map(v, table[3 * za], unit)
    v = apply_map(v, table[zb * (1 + za)], unit)
    v = apply_map(v, gath[zc * (z - 1) + (1 - zc) * NZ], unit)
    enter = column(v, unit)

    def block_states(b, _):
        e = jnp.sum(enter * bpre[b, pl.ds(0, S), :], axis=0, keepdims=True) + bpre[b, pl.ds(S, 1), :]
        e = jnp.broadcast_to(column(e, unit), (S, S))
        rows = [
            jnp.sum(e * pre_maps[b * L + step], axis=0, keepdims=True) + shifts[step, pl.ds(b, 1), :]
            for step in range(L)
        ]
        out = jnp.concatenate(rows, axis=0)
        states_out[pl.ds(pl.multiple_of(b * L, L), L), :] = out
        feats[head, pl.ds(pl.multiple_of(b * L, L), L), :] = out.astype(BF16)
        return 0

    lax.fori_loop(0, NB, block_states, 0)

    for q in peers:
        head_copy(q, feats.at[head], feats.at[head], f_send, f_recv).start()
    pre = jnp.zeros(hgrad.shape, F32)
    for dx in [0, 1, nx - 1, 2] if nx >= 4 else range(nx):
        for q in ((dx, 1), (dx, 0)):
            if q != (0, 0):
                head_copy(q, feats.at[head], feats.at[back(q)], f_send, f_recv).wait_recv()
        chip = lax.rem(x + nx - dx, nx)
        both = jnp.concatenate([feats[2 * chip], feats[2 * chip + 1]], axis=1)
        pre = pre + jnp.dot(
            both, w_up[pl.ds(pl.multiple_of(chip * 2 * S, 2 * S), 2 * S), :], preferred_element_type=F32
        )
        ftrans[pl.ds(pl.multiple_of(chip * 2 * S, 2 * S), 2 * S), :] = both.astype(F32).T.astype(BF16)
    gate = jax.nn.sigmoid(pre)
    hidden = (pre * gate).astype(BF16)
    pgrad = (hgrad[...] * gate * (1.0 + pre * (1.0 - gate))).astype(BF16)

    rows = S * nhead // ny
    share = rows // NZ
    for i in range(ny):
        out = jnp.dot(ctrans[pl.ds(i * rows, rows), :], hidden, preferred_element_type=F32).astype(BF16)
        for j in range(NZ):
            dblk[j, pl.ds(i * share, share)] = out[j * share : (j + 1) * share]
    ring_b1 = Ring(NZ, z, along_z, dblk, lb1, b1s, b1r, ny * share // 2)
    ring_b1.begin()
    for i in range(ny):
        ublk[i] = jnp.dot(ftrans[pl.ds(i * rows, rows), :], pgrad, preferred_element_type=F32).astype(BF16)
    ring_a1 = Ring(ny, y, along_y, ublk, la1, a1s, a1r, rows // 2)
    ring_a1.begin()

    for h in range(nhead):
        parts[h, 0] = dot_t(hidden, w_down[pl.ds(h * S, S), :]).astype(BF16)
        parts[h, 1] = dot_t(pgrad, w_up[pl.ds(h * S, S), :]).astype(BF16)
    for q in peers:
        head_copy(q, parts.at[peer(q)], landed.at[head], o_send, o_recv).start()

    ring_b1.advance(0)
    ring_a1.advance(0)
    ring_b1.advance(1)
    ring_a1.advance(1)
    half = rows // 2
    for c in range(2):
        out = ring_a1.total(c).astype(BF16)
        for j in range(NZ // 2):
            u2blk[c * (NZ // 2) + j] = out[j * share : (j + 1) * share]
    ring_a2 = Ring(NZ, z, along_z, u2blk, la2, a2s, a2r, share // 2)
    ring_a2.begin()
    ring_b1.advance(2)
    ring_a2.advance(0)
    ring_b1.advance(3)
    for c in range(2):
        out = ring_b1.total(c).astype(BF16)
        for j in range(ny // 2):
            d2blk[c * (ny // 2) + j] = out[j * share : (j + 1) * share]
    ring_b2 = Ring(ny, y, along_y, d2blk, lb2, b2s, b2r, share // 2)
    ring_b2.begin()
    ring_a2.advance(1)

    for q in peers:
        head_copy(q, parts.at[peer(q)], landed.at[back(q)], o_send, o_recv).wait_recv()
    outs = [parts[head, i].astype(F32) for i in range(2)]
    for q in peers:
        outs = [outs[i] + landed[back(q), i].astype(F32) for i in range(2)]
    mlp_out[...] = outs[0].astype(BF16)
    sgrad_out[...] = outs[1].astype(BF16)

    ring_b2.advance(0)
    ring_a2.advance(2)
    ring_b2.advance(1)
    ring_a2.advance(3)
    for c in range(2):
        gup_out[pl.ds(c * (share // 2), share // 2), :] = ring_a2.total(c)
        gdown_out[pl.ds(c * (share // 2), share // 2), :] = ring_b2.total(c)

    row_copy.wait_send()
    for q in peers:
        head_copy(q, cot, cots.at[head], c_send, c_recv).wait_send()
        head_copy(q, feats.at[head], feats.at[head], f_send, f_recv).wait_send()
        head_copy(q, parts.at[peer(q)], landed.at[head], o_send, o_recv).wait_send()
    for k in range(NZ // 2):
        for d in range(2):
            for c in range(2):
                if goes(d, k, c):
                    hop(d, k, c).wait_send()

    @pl.when(y < ny - 1)
    def _():
        chain.wait_send()

    for ring in (ring_a1, ring_a2, ring_b1, ring_b2):
        ring.finish()


def on_device(ntok, nhead, guess, drive, decay, mixing, init_state, skew_gen, w_up, w_down, cotangent):
    ny = ntok // NZ
    width, ff = w_up.shape
    share = width // ntok
    vm = pl.BlockSpec(memory_space=pltpu.VMEM)
    dma = pltpu.SemaphoreType.DMA
    landing = lambda n, half: pltpu.VMEM((2, n // 2, 2, half, ff), BF16)
    sems = lambda n: dma((2, n // 2, 2))
    scratch = [
        pltpu.VMEM((width, ff), BF16),
        pltpu.VMEM((width, ff), BF16),
        dma((2,)),
        pltpu.VMEM((S + 8, S), F32),
        dma,
        dma,
        pltpu.VMEM((S, S), F32),
        pltpu.VMEM((2 * S, 2 * S), BF16),
        pltpu.VMEM((S, S), F32),
        pltpu.VMEM((S, S), F32),
        pltpu.VMEM((S, S, S), F32),
        pltpu.VMEM((L, NB, S), F32),
        pltpu.VMEM((4, MR, S), F32),
        pltpu.VMEM((NB, MR, S), F32),
        pltpu.VMEM((NZ + 1, MR, S), F32),
        dma((2, NZ // 2, 2)),
        dma((2, NZ // 2, 2)),
        pltpu.VMEM((4, MR, S), F32),
        pltpu.VMEM((8, S), F32),
        pltpu.VMEM((8, S), F32),
        dma,
        dma,
        pltpu.VMEM((nhead, S, S), BF16),
        dma((nhead,)),
        dma((nhead,)),
        pltpu.VMEM((nhead, S, S), BF16),
        dma((nhead,)),
        dma((nhead,)),
        pltpu.VMEM((S, ff), F32),
        pltpu.VMEM((width, S), BF16),
        pltpu.VMEM((width, S), BF16),
        pltpu.VMEM((nhead, 2, S, S), BF16),
        pltpu.VMEM((nhead, 2, S, S), BF16),
        dma((nhead,)),
        dma((nhead,)),
        pltpu.VMEM((ny, NZ * share, ff), BF16),
        pltpu.VMEM((NZ, ny * share, ff), BF16),
        pltpu.VMEM((NZ, share, ff), BF16),
        pltpu.VMEM((ny, share, ff), BF16),
        landing(ny, NZ * share // 2),
        landing(NZ, share // 2),
        landing(NZ, ny * share // 2),
        landing(ny, share // 2),
        sems(ny),
        sems(ny),
        sems(NZ),
        sems(NZ),
        sems(NZ),
        sems(NZ),
        sems(ny),
        sems(ny),
    ]
    return pl.pallas_call(
        functools.partial(kernel, ntok, nhead),
        out_shape=(
            jax.ShapeDtypeStruct((S, S), F32),
            jax.ShapeDtypeStruct((S, S), BF16),
            jax.ShapeDtypeStruct((S, S), BF16),
            jax.ShapeDtypeStruct((share, ff), F32),
            jax.ShapeDtypeStruct((share, ff), F32),
        ),
        in_specs=[vm] * 6 + [pl.BlockSpec(memory_space=pl.ANY)] * 2 + [vm],
        out_specs=[vm] * 5,
        scratch_shapes=scratch,
        compiler_params=pltpu.CompilerParams(
            collective_id=0, has_side_effects=True, vmem_limit_bytes=56 * 1024 * 1024
        ),
    )(
        guess,
        drive,
        decay,
        mixing.reshape(1, S),
        init_state.reshape(1, S),
        skew_gen.reshape(S, S),
        w_up,
        w_down,
        cotangent,
    )


def solution(mesh):
    placed = (
        P("tok", "head"),
        P("tok", "head"),
        P("tok", "head"),
        P("head"),
        P("head"),
        P("head", None, None),
        P(None, "head"),
        P(None, "head"),
        P("tok", "head"),
    )
    return jax.shard_map(
        functools.partial(on_device, mesh.shape["tok"], mesh.shape["head"]),
        mesh=mesh,
        in_specs=placed,
        out_specs=(P("tok", "head"),) * 5,
        check_vma=False,
    )
```

time: 476 us -> 80.1 us (0.17)
  waiting for transfers between devices: 240 us -> 0 us
  matrix products: 107 us -> 0 us
  Pallas kernels: 0 us -> 74.4 us
  blocking collectives: 65.3 us -> 0 us
  other arithmetic: 28.5 us -> 0 us
  between operations: 14.1 us -> 0.66 us
  local copies, waits for them, and re-layouts: 9.27 us -> 4.22 us
    psum x1 -> x0, waiting for transfers between devices: 154 us -> none  [on_device(): lax.psum(up_terms.astype(jnp.bfloat16), 'tok').astype(jnp.float32)]
    dot_general x156 -> x0, matrix products: 107 us -> none  [the longest x35 34.8 us: combine_couple(): joined_map = jnp.dot(later[0], earlier[0], precision=exact_precision)]
    pallas_call x0 -> x1, Pallas kernels: none -> 74.4 us  [on_device(): pl.pallas_call(functools.partial(kernel, ntok, nhead), out_shape=(jax.Sha...]
    all_gather x3 -> x0, blocking collectives: 65.3 us -> none  [the longest x1 40.9 us: prefix(): pieces = jax.tree.map(lambda part: lax.all_gather(part, axis), value)]
    unnamed x6 -> x0, waiting for transfers between devices: 60.2 us -> none
    all_gather x1 -> x0, waiting for transfers between devices: 25.4 us -> none  [prefix(): pieces = jax.tree.map(lambda part: lax.all_gather(part, axis), value)]
    another operation x5 -> x0, other arithmetic: 22.9 us -> none  [the longest x3 12.4 us: cayley(): factor = jnp.linalg.cholesky(shifted)]
  transfers between devices with their start and end apart: 5 -> 0, of which waited for: 4 -> 0; matrix products, arithmetic and copies ran while one was open for 7% -> 0% of each run, Pallas kernels for 0% -> 0%
where the time goes in v1:
time: 80.1 us; the launch traced here: 79.3 us
  Pallas kernels  74.4 us (93%)
  local copies, waits for them, and re-layouts  4.22 us (5%)
    pallas_call x1, Pallas kernels, on_device(): pl.pallas_call(functools.partial(kernel, ntok, nhead), out_shape=(jax.Sha...  74.4 us
    unnamed x13, local copies, waits for them, and re-layouts  4.22 us

profile of v1, /device:TPU:8, one launch (start us, length us, event | category | flops | bytes accessed | tf_op | source)
XLA Modules:
  0.0 79.3 jit_solution(739675143542767984)
XLA Ops:
  0.6 74.4 %shard_map.128 = (f32[128,128]{1,0:T(8,128)}, bf16[128,128]{1,0:T(8,128)(2,1)}, bf16[128,128]{1,0:T(8,128)(2,1)}, f32[32,512]{1,0:T(8,128)}, f32[32,512]{1,0:T(8,128)}) custom-call(f32[128,128]{1,0:T(8,128)} %guess.1, f32[128,128]{1,0:T(8,128)} %drive.1, f32[128,128]{1,0:T(8,128)} %decay.1, f32[1,128]{1,0:T(1,128)} %bitcast.4, f32[1,128]{1,0:T(1,128)} %bitcast.5, ...), custom_call_target="tpu_custom_call" | custom-call | tf_op jit(solution)/shard_map/pallas_call | solution.py:607
  75.0 0.0 copy-start.3
  75.0 0.0 copy-start.2
  75.1 1.5 %copy.19 = f32[128,128]{1,0:T(8,128)} copy(f32[128,128]{1,0:T(8,128)} %get-tuple-element.10) | data formatting | bytes 131072
  76.5 0.0 copy-done.3
  76.5 0.0 copy-start.1
  76.5 0.6 copy.20
  77.2 0.0 copy-done.2
  77.2 0.6 copy.21
  77.8 0.0 copy-done.1
  77.8 0.0 copy-start
  77.8 0.6 copy.22
  78.4 0.2 copy-done
  78.6 0.6 copy.23
Async XLA Ops:
  75.0 1.5 %copy-start.3 = (bf16[128,128]{1,0:T(8,128)(2,1)S(1)}, bf16[128,128]{1,0:T(8,128)(2,1)}, u32[]{:S(2)}) copy-start(bf16[128,128]{1,0:T(8,128)(2,1)} %get-tuple-element.11) | copy-start | bytes 98308
  75.0 2.1 %copy-start.2 = (bf16[128,128]{1,0:T(8,128)(2,1)S(1)}, bf16[128,128]{1,0:T(8,128)(2,1)}, u32[]{:S(2)}) copy-start(bf16[128,128]{1,0:T(8,128)(2,1)} %get-tuple-element.12) | copy-start | bytes 98308
  76.5 1.2 %copy-start.1 = (f32[32,512]{1,0:T(8,128)S(1)}, f32[32,512]{1,0:T(8,128)}, u32[]{:S(2)}) copy-start(f32[32,512]{1,0:T(8,128)} %get-tuple-element.13) | copy-start | bytes 196612
  77.8 0.9 %copy-start = (f32[32,512]{1,0:T(8,128)S(1)}, f32[32,512]{1,0:T(8,128)}, u32[]{:S(2)}) copy-start(f32[32,512]{1,0:T(8,128)} %get-tuple-element.14) | copy-start | bytes 196612

commit v2 on v1

v2 whole, which is shorter than its diff:
```python
import functools

import jax
import jax.numpy as jnp
from jax import lax
from jax.experimental import pallas as pl
from jax.experimental.pallas import tpu as pltpu
from jax.sharding import PartitionSpec as P

MESH = pl.DeviceIdType.MESH
F32, BF16 = jnp.float32, jnp.bfloat16
S = 128
NZ = 8
NB, L = 8, 16
MR = 144
SENT = 136
CUTS = ((0, 40), (40, 32), (72, 32), (104, 32))
NEWTON = 14
PIECES = 4
ORDER = (4, 3, 6, 1, 5, 2, 7, 0)
TURN = (2, 3, 1, 0)


def split(x):
    hi = x.astype(BF16)
    return hi, (x - hi.astype(F32)).astype(BF16)


def left(x):
    return jnp.concatenate(split(x), axis=1)


def right(x):
    both = jnp.concatenate(split(x), axis=1)
    return jnp.concatenate([both, both], axis=0)


def product(l, r):
    out = jnp.dot(l, r, preferred_element_type=F32)
    return out[:, :S] + out[:, S:]


def mm(a, b):
    return product(left(a), right(b))


def compose(first, then):
    out = mm(first, then[:S])
    return jnp.concatenate([out[:S], out[S:] + then[S:]], axis=0)


def eye():
    rows = lax.broadcasted_iota(jnp.int32, (S, S), 0)
    cols = lax.broadcasted_iota(jnp.int32, (S, S), 1)
    return jnp.where(rows == cols, 1.0, 0.0).astype(F32)


def column(v, unit):
    return jnp.sum(unit * v, axis=1, keepdims=True)


def apply_map(v, m, unit):
    return jnp.sum(column(v, unit) * m[:S], axis=0, keepdims=True) + m[S : S + 1]


def dot_t(a, b):
    return lax.dot_general(a, b, (((1,), (1,)), ((), ())), preferred_element_type=F32)


class Ring:
    def __init__(self, n, me, device, blocks, landing, send, recv):
        self.n, self.me, self.device = n, me, device
        self.blocks, self.landing, self.send, self.recv = blocks, landing, send, recv
        self.rows = blocks.shape[1] // PIECES

    def owner(self, d, hop):
        way = 1 if d == 0 else -1
        return lax.rem(self.me + way * (self.n // 2 - hop) + 2 * self.n, self.n)

    def at(self, c):
        return pl.ds(c * self.rows, self.rows)

    def copy(self, d, hop, c):
        target = lax.rem(self.me + (1 if d == 0 else -1) + self.n, self.n)
        return pltpu.make_async_remote_copy(
            src_ref=self.blocks.at[self.owner(d, hop), self.at(c)],
            dst_ref=self.landing.at[d, hop, c],
            send_sem=self.send.at[d, hop, c],
            recv_sem=self.recv.at[d, hop, c],
            device_id=self.device(target),
            device_id_type=MESH,
        )

    @staticmethod
    def first(d):
        return (0, 1) if d == 0 else (2, 3)

    def begin(self):
        for i in range(2):
            for d in range(2):
                self.copy(d, 0, self.first(d)[i]).start()
        for i in range(2):
            for d in range(2):
                self.copy(d, 1, self.first(1 - d)[i]).start()

    def advance(self, hop, early):
        for i in range(2):
            for d in range(2):
                c = self.first(1 - d if early else d)[i]
                self.copy(d, hop, c).wait_recv()
                to = self.owner(d, hop + 1)
                self.blocks[to, self.at(c)] = (
                    self.blocks[to, self.at(c)].astype(F32) + self.landing[d, hop, c].astype(F32)
                ).astype(BF16)
                self.copy(d, hop + 1, c).start()

    def total(self, c):
        last = self.n // 2 - 1
        out = self.blocks[self.me, self.at(c)].astype(F32)
        for d in range(2):
            self.copy(d, last, c).wait_recv()
            out = out + self.landing[d, last, c].astype(F32)
        return out

    def finish(self):
        for hop in range(self.n // 2):
            for d in range(2):
                for c in self.first(d) if hop == 0 else range(PIECES):
                    self.copy(d, hop, c).wait_send()


def kernel(
    ntok,
    nhead,
    guess,
    drive,
    decay,
    mixing,
    init,
    skew,
    w_up_hbm,
    w_down_hbm,
    cot,
    states_out,
    mlp_out,
    sgrad_out,
    gup_out,
    gdown_out,
    w_up,
    w_down,
    w_sem,
    shifted,
    row_send,
    row_recv,
    wrot,
    slopes,
    offs,
    pre_maps,
    shifts,
    bmaps,
    bpre,
    gath,
    gsend,
    grecv,
    table,
    vin,
    vout,
    tin,
    tout,
    v_send,
    v_recv,
    feats,
    f_send,
    f_recv,
    cots,
    c_send,
    c_recv,
    hgrad,
    hidden,
    pgrad,
    ftrans,
    ctrans,
    parts,
    landed,
    o_send,
    o_recv,
    ublk,
    dblk,
    u2blk,
    d2blk,
    la1,
    la2,
    lb1,
    lb2,
    a1s,
    a1r,
    a2s,
    a2r,
    b1s,
    b1r,
    b2s,
    b2r,
):
    ny, nx = ntok // NZ, nhead // 2
    tok, head = lax.axis_index("tok"), lax.axis_index("head")
    y, z = lax.div(tok, NZ), lax.rem(tok, NZ)
    x, core = lax.div(head, 2), lax.rem(head, 2)

    def along_z(target):
        return {"tok": y * NZ + target, "head": head}

    def along_y(target):
        return {"tok": target * NZ + z, "head": head}

    def at_tok(target):
        return {"tok": target, "head": head}

    def at_head(target):
        return {"tok": tok, "head": target}

    peers = [(dx, flip) for dx in ([0, 1, nx - 1, 2] if nx >= 4 else range(nx)) for flip in (1, 0)]
    peers = [q for q in peers if q != (0, 0)]

    def peer(q):
        return lax.rem(x + q[0], nx) * 2 + lax.rem(core + q[1], 2)

    after, before_me = lax.rem(tok + 1, ntok), lax.rem(tok + ntok - 1, ntok)

    barrier = pltpu.get_barrier_semaphore()
    greet = [along_z(lax.rem(z + 1, NZ)), along_z(lax.rem(z + NZ - 1, NZ))]
    greet += [along_y(lax.rem(y + i, ny)) for i in range(1, ny)]
    greet += [at_tok(after), at_tok(before_me)]
    greet += [at_head(peer(q)) for q in peers]
    for who in greet:
        pl.semaphore_signal(barrier, inc=1, device_id=who, device_id_type=MESH)
    loads = [
        pltpu.make_async_copy(w_up_hbm, w_up, w_sem.at[0]),
        pltpu.make_async_copy(w_down_hbm, w_down, w_sem.at[1]),
    ]
    for load in loads:
        load.start()

    unit = eye()
    k = skew[...]
    a = unit + k
    kk = mm(k, k)
    bound = jnp.sqrt(jnp.sum(jnp.sum(kk * kk, axis=1, keepdims=True), axis=0, keepdims=True) * 0.5)
    top = 1.0 + 1.01 * bound
    scale = 2.0 / (1.0 + top)
    gap = (top - 1.0) / (top + 1.0)

    def newton(v, t, gap):
        square = gap * gap
        wide = 2.0 / (2.0 - square)
        out = product(left(jnp.concatenate([t, v], axis=0)), right(wide * (2.0 * unit - t)))
        return out[S:], out[:S], square / (2.0 - square)

    v, t = (unit - k) * scale, (unit - kk) * scale
    for _ in range(NEWTON // 2):
        v, t, gap = newton(v, t, gap)

    pl.semaphore_wait(barrier, len(greet))
    row_copy = pltpu.make_async_remote_copy(
        src_ref=guess.at[pl.ds(S - 8, 8)],
        dst_ref=shifted.at[pl.ds(0, 8)],
        send_sem=row_send,
        recv_sem=row_recv,
        device_id=at_tok(after),
        device_id_type=MESH,
    )
    row_copy.start()

    def head_copy(q, src, dst, send, recv):
        return pltpu.make_async_remote_copy(
            src_ref=src,
            dst_ref=dst,
            send_sem=send.at[q[0] * 2 + q[1]],
            recv_sem=recv.at[q[0] * 2 + q[1]],
            device_id=at_head(peer(q)),
            device_id_type=MESH,
        )

    def back(q):
        return lax.rem(x + nx - q[0], nx) * 2 + lax.rem(core + q[1], 2)

    for q in peers:
        head_copy(q, cot, cots.at[head], c_send, c_recv).start()
    cots[head] = cot[...]

    for _ in range(NEWTON - NEWTON // 2):
        v, t, gap = newton(v, t, gap)
    t = jnp.dot(a, v, precision=lax.Precision.HIGHEST, preferred_element_type=F32)
    v = v + mm(v, unit - t)
    rot_t = 2.0 * v - unit
    wrot[...] = right(rot_t)

    shifted[pl.ds(8, S), :] = guess[...]
    row_copy.wait_recv()
    before = shifted[pl.ds(7, S), :]
    first = (lax.broadcasted_iota(jnp.int32, (S, S), 0) == 0) & (tok == 0)
    before = jnp.where(first, init[...], before)
    m = mixing[...]
    bent = jnp.tanh(before)
    curve = 1.0 - bent * bent
    slopes[...] = (1.0 - m) * decay[...] + m * curve
    offs[...] = product(left(m * (bent - curve * before)), wrot[...]) + drive[...]

    def advance(step, blocks, shift):
        rows = [left(blocks[b] * slopes[pl.ds(b * L + step, 1), :]) for b in range(NB)]
        shift = shift * slopes[pl.ds(step, NB, stride=L), :]
        rows.append(left(jnp.concatenate([shift, jnp.zeros((16 - NB, S), F32)], axis=0)))
        out = product(jnp.concatenate(rows, axis=0), wrot[...])
        for b in range(NB):
            pre_maps[b * L + step] = out[b * S : (b + 1) * S]
        shifts[step] = out[NB * S : NB * S + NB] + offs[pl.ds(step, NB, stride=L), :]

    advance(0, [unit] * NB, jnp.zeros((NB, S), F32))

    for step in range(1, L):
        advance(step, [pre_maps[b * L + step - 1] for b in range(NB)], shifts[step - 1])

    pad = jnp.zeros((MR - S - 1, S), F32)

    def block_map(b):
        return jnp.concatenate([pre_maps[b * L + L - 1], shifts[L - 1, b : b + 1], pad], axis=0)

    none = jnp.concatenate([unit, jnp.zeros((MR - S, S), F32)], axis=0)
    bpre[0] = none
    bpre[1] = block_map(0)
    bpre[2] = compose(block_map(0), block_map(1))
    bmaps[0] = compose(block_map(2), block_map(3))
    bmaps[1] = compose(block_map(4), block_map(5))
    bmaps[2] = compose(block_map(6), block_map(7))
    bpre[4] = compose(bpre[2], bmaps[0])
    bmaps[3] = compose(bmaps[1], bmaps[2])
    gath[z] = compose(bpre[4], bmaps[3])

    def hop(d, k, c, arriving=0):
        way = 1 if d == 0 else -1
        part = gath.at[lax.rem(z - way * (k + arriving) + 2 * NZ, NZ), pl.ds(*CUTS[c])]
        return pltpu.make_async_remote_copy(
            src_ref=part,
            dst_ref=part,
            send_sem=gsend.at[d, k, c],
            recv_sem=grecv.at[d, k, c],
            device_id=along_z(lax.rem(z + way + NZ, NZ)),
            device_id_type=MESH,
        )

    def goes(d, k, c):
        return k < NZ // 2 - 1 or c // 2 == d

    turns = [(d, c if d == 0 else (c + 2) % 4) for c in range(4) for d in range(2)]
    for d, c in turns:
        hop(d, 0, c).start()

    def relay(k):
        for d, c in turns:
            if goes(d, k, c):
                hop(d, k, c, 1).wait_recv()
                if k + 1 < NZ // 2 and goes(d, k + 1, c):
                    hop(d, k + 1, c).start()

    for load in loads:
        load.wait()
    for q in peers:
        head_copy(q, cot, cots.at[back(q)], c_send, c_recv).wait_recv()
    hgrad[...] = jnp.zeros_like(hgrad)
    for c in range(nx):
        hgrad[...] += jnp.dot(
            jnp.concatenate([cots[2 * c], cots[2 * c + 1]], axis=1),
            w_down[pl.ds(c * 2 * S, 2 * S), :],
            preferred_element_type=F32,
        )
    relay(0)
    for h in range(nhead):
        ctrans[pl.ds(h * S, S), :] = cots[h].astype(F32).T.astype(BF16)
    bpre[3] = compose(bpre[2], block_map(2))
    bpre[5] = compose(bpre[4], block_map(4))
    relay(1)
    bpre[6] = compose(bpre[4], bmaps[1])
    bpre[7] = compose(bpre[6], block_map(6))
    gath[NZ] = none
    table[0] = none
    relay(2)
    relay(3)
    pairs = [compose(gath[2 * i], gath[2 * i + 1]) for i in range(4)]
    table[1] = pairs[0]
    table[2] = pairs[2]
    low = compose(pairs[0], pairs[1])
    table[3] = low
    whole = compose(low, compose(pairs[2], pairs[3]))

    def chain(i, target):
        return pltpu.make_async_remote_copy(
            src_ref=vout,
            dst_ref=vin,
            send_sem=v_send.at[i],
            recv_sem=v_recv.at[0],
            device_id=along_y(target),
            device_id_type=MESH,
        )

    carry = pltpu.make_async_remote_copy(
        src_ref=tout.at[pl.ds(0, SENT)],
        dst_ref=tin.at[pl.ds(0, SENT)],
        send_sem=v_send.at[2],
        recv_sem=v_recv.at[1],
        device_id=along_y(3),
        device_id_type=MESH,
    )

    @pl.when(y == 2)
    def _():
        tout[...] = whole
        carry.start()

    @pl.when(y == 0)
    def _():
        vin[...] = jnp.broadcast_to(init[...], (8, S))
        vout[...] = jnp.broadcast_to(apply_map(init[...], whole, unit), (8, S))
        chain(0, 1).start()

    @pl.when(y > 0)
    def _():
        chain(0, 1).wait_recv()

    @pl.when(y == 1)
    def _():
        vout[...] = jnp.broadcast_to(apply_map(vin[0:1, :], whole, unit), (8, S))
        chain(0, 3).start()
        chain(1, 2).start()

    @pl.when(y == 3)
    def _():
        carry.wait_recv()
        vin[...] = jnp.broadcast_to(apply_map(vin[0:1, :], tin, unit), (8, S))

    v = vin[0:1, :]
    za, zb, zc = lax.div(z, 4), lax.rem(lax.div(z, 2), 2), lax.rem(z, 2)
    v = apply_map(v, table[3 * za], unit)
    v = apply_map(v, table[zb * (1 + za)], unit)
    v = apply_map(v, gath[zc * (z - 1) + (1 - zc) * NZ], unit)
    enter = column(v, unit)

    half = S // 2

    def feat_copy(q, part, who):
        return pltpu.make_async_remote_copy(
            src_ref=feats.at[head, pl.ds(part * half, half)],
            dst_ref=feats.at[who, pl.ds(part * half, half)],
            send_sem=f_send.at[part, q[0] * 2 + q[1]],
            recv_sem=f_recv.at[part, q[0] * 2 + q[1]],
            device_id=at_head(peer(q)),
            device_id_type=MESH,
        )

    for b in range(NB):
        e = jnp.sum(enter * bpre[b, 0:S, :], axis=0, keepdims=True) + bpre[b, S : S + 1, :]
        e = jnp.broadcast_to(column(e, unit), (S, S))
        rows = [
            jnp.sum(e * pre_maps[b * L + step], axis=0, keepdims=True) + shifts[step, b : b + 1, :]
            for step in range(L)
        ]
        out = jnp.concatenate(rows, axis=0)
        states_out[b * L : (b + 1) * L, :] = out
        feats[head, b * L : (b + 1) * L, :] = out.astype(BF16)
        if b % (NB // 2) == NB // 2 - 1:
            for q in peers:
                feat_copy(q, b // (NB // 2), head).start()

    def of_chip(dx, rows):
        chip = lax.rem(x + nx - dx, nx)
        both = jnp.concatenate([feats[2 * chip, rows], feats[2 * chip + 1, rows]], axis=1)
        return both, pl.ds(pl.multiple_of(chip * 2 * S, 2 * S), 2 * S)

    ring_dx = [0, 1, nx - 1, 2]
    for part in range(2):
        rows = slice(part * half, (part + 1) * half)
        pre = jnp.zeros((half, w_up.shape[1]), F32)
        for dx in ring_dx:
            for q in ((dx, 1), (dx, 0)):
                if q != (0, 0):
                    feat_copy(q, part, back(q)).wait_recv()
            both, cols = of_chip(dx, rows)
            pre = pre + jnp.dot(both, w_up[cols, :], preferred_element_type=F32)
        gate = jax.nn.sigmoid(pre)
        hidden[rows, :] = (pre * gate).astype(BF16)
        pgrad[rows, :] = (hgrad[rows, :] * gate * (1.0 + pre * (1.0 - gate))).astype(BF16)

    rows = S * nhead // ny
    share = rows // NZ
    for i in range(ny):
        out = jnp.dot(ctrans[pl.ds(i * rows, rows), :], hidden[...], preferred_element_type=F32).astype(BF16)
        place = lax.rem(i - y + ny, ny)
        piece = sum(jnp.where(place == t, n, 0) for n, t in enumerate(TURN))
        for j in range(NZ):
            dblk[j, pl.ds(pl.multiple_of(piece * share, share), share)] = out[j * share : (j + 1) * share]
    ring_b1 = Ring(NZ, z, along_z, dblk, lb1, b1s, b1r)
    ring_b1.begin()
    for dx in ring_dx:
        both, cols = of_chip(dx, slice(0, S))
        ftrans[cols, :] = both.astype(F32).T.astype(BF16)
    for i in range(ny):
        out = jnp.dot(ftrans[pl.ds(i * rows, rows), :], pgrad[...], preferred_element_type=F32).astype(BF16)
        for j in range(NZ):
            place = lax.rem(j - z + NZ, NZ)
            piece = sum(jnp.where(place == t, n, 0) for n, t in enumerate(ORDER))
            ublk[i, pl.ds(pl.multiple_of(piece * share, share), share)] = out[j * share : (j + 1) * share]
    ring_a1 = Ring(ny, y, along_y, ublk, la1, a1s, a1r)
    ring_a1.begin()

    for h in range(nhead):
        parts[h, 0] = dot_t(hidden[...], w_down[pl.ds(h * S, S), :]).astype(BF16)
        parts[h, 1] = dot_t(pgrad[...], w_up[pl.ds(h * S, S), :]).astype(BF16)
    for q in peers:
        head_copy(q, parts.at[peer(q)], landed.at[head], o_send, o_recv).start()

    def up_copy(r):
        return pltpu.make_async_remote_copy(
            src_ref=u2blk.at[r],
            dst_ref=la2.at[r],
            send_sem=a2s.at[r],
            recv_sem=a2r.at[r],
            device_id=along_z(lax.rem(z + r, NZ)),
            device_id_type=MESH,
        )

    def up_part(c):
        out = ring_a1.total(c)
        for i in range(2):
            r = ORDER[2 * c + i]
            mine = out[i * share : (i + 1) * share]
            if r == 0:
                gup_out[...] = mine
            else:
                u2blk[r] = mine.astype(BF16)
                up_copy(r).start()

    def down_copy(r):
        return pltpu.make_async_remote_copy(
            src_ref=d2blk.at[r],
            dst_ref=lb2.at[r],
            send_sem=b2s.at[r],
            recv_sem=b2r.at[r],
            device_id=along_y(lax.rem(y + r, ny)),
            device_id_type=MESH,
        )

    def down_part(c):
        out = ring_b1.total(c)
        r = TURN[c]
        if r == 0:
            gdown_out[...] = out
        else:
            d2blk[r] = out.astype(BF16)
            down_copy(r).start()

    ring_b1.advance(0, False)
    ring_a1.advance(0, False)
    ring_b1.advance(1, True)
    ring_b1.advance(1, False)
    ring_b1.advance(2, True)
    ring_b1.advance(2, False)
    for q in peers:
        head_copy(q, parts.at[peer(q)], landed.at[back(q)], o_send, o_recv).wait_recv()
    outs = [parts[head, i].astype(F32) for i in range(2)]
    for q in peers:
        outs = [outs[i] + landed[back(q), i].astype(F32) for i in range(2)]
    mlp_out[...] = outs[0].astype(BF16)
    sgrad_out[...] = outs[1].astype(BF16)
    up_part(0)
    up_part(2)
    up_part(1)
    up_part(3)
    for c in (0, 2, 1, 3):
        down_part(c)
    for r in (1, 7, 2, 6, 3, 5, 4):
        up_copy(r).wait_recv()
        gup_out[...] += la2[r].astype(F32)
    for r in (1, 3, 2):
        down_copy(r).wait_recv()
        gdown_out[...] += lb2[r].astype(F32)

    row_copy.wait_send()
    for q in peers:
        head_copy(q, cot, cots.at[head], c_send, c_recv).wait_send()
        for part in range(2):
            feat_copy(q, part, head).wait_send()
        head_copy(q, parts.at[peer(q)], landed.at[head], o_send, o_recv).wait_send()
    for k in range(NZ // 2):
        for d in range(2):
            for c in range(len(CUTS)):
                if goes(d, k, c):
                    hop(d, k, c).wait_send()

    @pl.when(y < 2)
    def _():
        chain(0, 1).wait_send()

    @pl.when(y == 1)
    def _():
        chain(1, 2).wait_send()

    @pl.when(y == 2)
    def _():
        carry.wait_send()

    for ring in (ring_a1, ring_b1):
        ring.finish()
    for r in range(1, NZ):
        up_copy(r).wait_send()
    for r in range(1, ny):
        down_copy(r).wait_send()


def settle(*refs):
    for src, dst in zip(refs[:5], refs[5:]):
        dst[...] = src[...]


def on_device(ntok, nhead, guess, drive, decay, mixing, init_state, skew_gen, w_up, w_down, cotangent):
    ny = ntok // NZ
    width, ff = w_up.shape
    share = width // ntok
    vm = pl.BlockSpec(memory_space=pltpu.VMEM)
    dma = pltpu.SemaphoreType.DMA
    landing = lambda n, rows: pltpu.VMEM((2, n // 2, PIECES, rows // PIECES, ff), BF16)
    sems = lambda n: dma((2, n // 2, PIECES))
    scratch = [
        pltpu.VMEM((width, ff), BF16),
        pltpu.VMEM((width, ff), BF16),
        dma((2,)),
        pltpu.VMEM((S + 8, S), F32),
        dma,
        dma,
        pltpu.VMEM((2 * S, 2 * S), BF16),
        pltpu.VMEM((S, S), F32),
        pltpu.VMEM((S, S), F32),
        pltpu.VMEM((S, S, S), F32),
        pltpu.VMEM((L, NB, S), F32),
        pltpu.VMEM((4, MR, S), F32),
        pltpu.VMEM((NB, MR, S), F32),
        pltpu.VMEM((NZ + 1, MR, S), F32),
        dma((2, NZ // 2, len(CUTS))),
        dma((2, NZ // 2, len(CUTS))),
        pltpu.VMEM((4, MR, S), F32),
        pltpu.VMEM((8, S), F32),
        pltpu.VMEM((8, S), F32),
        pltpu.VMEM((MR, S), F32),
        pltpu.VMEM((MR, S), F32),
        dma((3,)),
        dma((2,)),
        pltpu.VMEM((nhead, S, S), BF16),
        dma((2, nhead)),
        dma((2, nhead)),
        pltpu.VMEM((nhead, S, S), BF16),
        dma((nhead,)),
        dma((nhead,)),
        pltpu.VMEM((S, ff), F32),
        pltpu.VMEM((S, ff), BF16),
        pltpu.VMEM((S, ff), BF16),
        pltpu.VMEM((width, S), BF16),
        pltpu.VMEM((width, S), BF16),
        pltpu.VMEM((nhead, 2, S, S), BF16),
        pltpu.VMEM((nhead, 2, S, S), BF16),
        dma((nhead,)),
        dma((nhead,)),
        pltpu.VMEM((ny, NZ * share, ff), BF16),
        pltpu.VMEM((NZ, ny * share, ff), BF16),
        pltpu.VMEM((NZ, share, ff), BF16),
        pltpu.VMEM((ny, share, ff), BF16),
        landing(ny, NZ * share),
        pltpu.VMEM((NZ, share, ff), BF16),
        landing(NZ, ny * share),
        pltpu.VMEM((ny, share, ff), BF16),
        sems(ny),
        sems(ny),
        dma((NZ,)),
        dma((NZ,)),
        sems(NZ),
        sems(NZ),
        dma((ny,)),
        dma((ny,)),
    ]
    results = [((S, S), F32), ((S, S), BF16), ((S, S), BF16), ((share, ff), F32), ((share, ff), F32)]
    done = pl.pallas_call(
        functools.partial(kernel, ntok, nhead),
        out_shape=tuple(pltpu.VMEM(*r) for r in results),
        in_specs=[vm] * 6 + [pl.BlockSpec(memory_space=pl.ANY)] * 2 + [vm],
        out_specs=[vm] * 5,
        scratch_shapes=scratch,
        compiler_params=pltpu.CompilerParams(
            collective_id=0, has_side_effects=True, vmem_limit_bytes=56 * 1024 * 1024
        ),
    )(
        guess,
        drive,
        decay,
        mixing.reshape(1, S),
        init_state.reshape(1, S),
        skew_gen.reshape(S, S),
        w_up,
        w_down,
        cotangent,
    )
    return pl.pallas_call(
        settle,
        out_shape=tuple(jax.ShapeDtypeStruct(*r) for r in results),
        in_specs=[vm] * 5,
        out_specs=[vm] * 5,
    )(*[pltpu.with_memory_space_constraint(d, pltpu.VMEM) for d in done])


def solution(mesh):
    placed = (
        P("tok", "head"),
        P("tok", "head"),
        P("tok", "head"),
        P("head"),
        P("head"),
        P("head", None, None),
        P(None, "head"),
        P(None, "head"),
        P("tok", "head"),
    )
    return jax.shard_map(
        functools.partial(on_device, mesh.shape["tok"], mesh.shape["head"]),
        mesh=mesh,
        in_specs=placed,
        out_specs=(P("tok", "head"),) * 5,
        check_vma=False,
    )
```

time: 80.1 us -> 67.6 us (0.84)
  Pallas kernels: 74.4 us -> 66.8 us
  local copies, waits for them, and re-layouts: 4.22 us -> 0 us
    pallas_call x1 -> x2, Pallas kernels: 74.4 us -> 66.8 us  [the longest x1 66.1 us: on_device(): pl.pallas_call(functools.partial(kernel, ntok, nhead), out_shape=tuple((p...]
    unnamed x13 -> x0, local copies, waits for them, and re-layouts: 4.22 us -> none
where the time goes in v2:
time: 67.6 us; the launch traced here: 67.5 us
  Pallas kernels  66.8 us (99%)
    pallas_call x1, Pallas kernels, on_device(): pl.pallas_call(functools.partial(kernel, ntok, nhead), out_shape=tuple((p...  66.1 us

profile of v2, /device:TPU:8, one launch (start us, length us, event | category | flops | bytes accessed | tf_op | source)
XLA Modules:
  0.0 67.5 jit_solution(1504300155715538066)
XLA Ops:
  0.6 66.1 %shard_map.128 = (f32[128,128]{1,0:T(8,128)S(1)}, bf16[128,128]{1,0:T(8,128)(2,1)S(1)}, bf16[128,128]{1,0:T(8,128)(2,1)S(1)}, f32[32,512]{1,0:T(8,128)S(1)}, f32[32,512]{1,0:T(8,128)S(1)}) custom-call(f32[128,128]{1,0:T(8,128)} %guess.1, f32[128,128]{1,0:T(8,128)} %drive.1, f32[128,128]{1,0:T(8,128)} %decay.1, f32[1,128]{1,0:T(1,128)} %bitcast.4, ...), custom_call_target="tpu_custom_call" | custom-call | tf_op jit(solution)/shard_map/pallas_call | solution.py:687
  66.7 0.7 %shard_map.129 = (f32[128,128]{1,0:T(8,128)}, bf16[128,128]{1,0:T(8,128)(2,1)}, bf16[128,128]{1,0:T(8,128)(2,1)}, f32[32,512]{1,0:T(8,128)}, f32[32,512]{1,0:T(8,128)}) custom-call(f32[128,128]{1,0:T(8,128)S(1)} %get-tuple-element.10.refs_0_, bf16[128,128]{1,0:T(8,128)(2,1)S(1)} %get-tuple-element.11.refs_1_, ...), custom_call_target="tpu_custom_call" | custom-call | tf_op jit(solution)/shard_map/pallas_call | solution.py:707

commit v3 on v2

--- a/solution.py
+++ b/solution.py
@@ -14,7 +14,8 @@
 NB, L = 8, 16
 MR = 144
 SENT = 136
-CUTS = ((0, 40), (40, 32), (72, 32), (104, 32))
+CUTS = ((0, 72), (72, 64))
+LEGS = ((2, 0), (-2, 0), (1, 0), (-1, 0), (1, -2), (-1, 2), (2, -2), (-2, 2))
 NEWTON = 14
 PIECES = 4
 ORDER = (4, 3, 6, 1, 5, 2, 7, 0)
@@ -227,7 +228,7 @@
     after, before_me = lax.rem(tok + 1, ntok), lax.rem(tok + ntok - 1, ntok)
 
     barrier = pltpu.get_barrier_semaphore()
-    greet = [along_z(lax.rem(z + 1, NZ)), along_z(lax.rem(z + NZ - 1, NZ))]
+    greet = [along_z(lax.rem(z + i, NZ)) for i in (1, 2, NZ - 1, NZ - 2)]
     greet += [along_y(lax.rem(y + i, ny)) for i in range(1, ny)]
     greet += [at_tok(after), at_tok(before_me)]
     greet += [at_head(peer(q)) for q in peers]
@@ -335,31 +336,25 @@
     bmaps[3] = compose(bmaps[1], bmaps[2])
     gath[z] = compose(bpre[4], bmaps[3])
 
-    def hop(d, k, c, arriving=0):
-        way = 1 if d == 0 else -1
-        part = gath.at[lax.rem(z - way * (k + arriving) + 2 * NZ, NZ), pl.ds(*CUTS[c])]
+    def leg(n, c, arriving=False):
+        way, owner = LEGS[n]
+        owner = owner - way if arriving else owner
+        part = gath.at[lax.rem(z + owner + 2 * NZ, NZ), pl.ds(*CUTS[c])]
         return pltpu.make_async_remote_copy(
             src_ref=part,
             dst_ref=part,
-            send_sem=gsend.at[d, k, c],
-            recv_sem=grecv.at[d, k, c],
+            send_sem=gsend.at[n, c],
+            recv_sem=grecv.at[n, c],
             device_id=along_z(lax.rem(z + way + NZ, NZ)),
             device_id_type=MESH,
         )
 
-    def goes(d, k, c):
-        return k < NZ // 2 - 1 or c // 2 == d
-
-    turns = [(d, c if d == 0 else (c + 2) % 4) for c in range(4) for d in range(2)]
-    for d, c in turns:
-        hop(d, 0, c).start()
-
-    def relay(k):
-        for d, c in turns:
-            if goes(d, k, c):
-                hop(d, k, c, 1).wait_recv()
-                if k + 1 < NZ // 2 and goes(d, k + 1, c):
-                    hop(d, k + 1, c).start()
+    def legs(n):
+        return (n % 2,) if n >= 6 else (0, 1)
+
+    for n in range(4):
+        for c in legs(n):
+            leg(n, c).start()
 
     for load in loads:
         load.wait()
@@ -372,18 +367,23 @@
             w_down[pl.ds(c * 2 * S, 2 * S), :],
             preferred_element_type=F32,
         )
-    relay(0)
+    for c in range(2):
+        for n in range(2):
+            leg(n, c, True).wait_recv()
+            if c in legs(6 + n):
+                leg(6 + n, c).start()
+            leg(4 + n, c).start()
     for h in range(nhead):
         ctrans[pl.ds(h * S, S), :] = cots[h].astype(F32).T.astype(BF16)
     bpre[3] = compose(bpre[2], block_map(2))
     bpre[5] = compose(bpre[4], block_map(4))
-    relay(1)
     bpre[6] = compose(bpre[4], bmaps[1])
     bpre[7] = compose(bpre[6], block_map(6))
     gath[NZ] = none
     table[0] = none
-    relay(2)
-    relay(3)
+    for n in range(2, 8):
+        for c in legs(n):
+            leg(n, c, True).wait_recv()
     pairs = [compose(gath[2 * i], gath[2 * i + 1]) for i in range(4)]
     table[1] = pairs[0]
     table[2] = pairs[2]
@@ -391,50 +391,51 @@
     table[3] = low
     whole = compose(low, compose(pairs[2], pairs[3]))
 
-    def chain(i, target):
+    def tell_state(row):
         return pltpu.make_async_remote_copy(
             src_ref=vout,
             dst_ref=vin,
-            send_sem=v_send.at[i],
+            send_sem=v_send.at[row],
             recv_sem=v_recv.at[0],
-            device_id=along_y(target),
+            device_id=along_y(row),
             device_id_type=MESH,
         )
 
-    carry = pltpu.make_async_remote_copy(
-        src_ref=tout.at[pl.ds(0, SENT)],
-        dst_ref=tin.at[pl.ds(0, SENT)],
-        send_sem=v_send.at[2],
-        recv_sem=v_recv.at[1],
-        device_id=along_y(3),
-        device_id_type=MESH,
-    )
-
-    @pl.when(y == 2)
-    def _():
-        tout[...] = whole
-        carry.start()
+    def tell_map(row, owner):
+        return pltpu.make_async_remote_copy(
+            src_ref=tout.at[pl.ds(0, SENT)],
+            dst_ref=tin.at[owner - 1, pl.ds(0, SENT)],
+            send_sem=v_send.at[row],
+            recv_sem=v_recv.at[owner],
+            device_id=along_y(row),
+            device_id_type=MESH,
+        )
 
     @pl.when(y == 0)
     def _():
+        vout[...] = jnp.broadcast_to(apply_map(init[...], whole, unit), (8, S))
+        for row in range(ny - 1, 0, -1):
+            tell_state(row).start()
         vin[...] = jnp.broadcast_to(init[...], (8, S))
-        vout[...] = jnp.broadcast_to(apply_map(init[...], whole, unit), (8, S))
-        chain(0, 1).start()
+
+    for owner in range(1, ny - 1):
+
+        @pl.when(y == owner)
+        def _():
+            tout[...] = whole
+            for row in range(ny - 1, owner, -1):
+                tell_map(row, owner).start()
 
     @pl.when(y > 0)
     def _():
-        chain(0, 1).wait_recv()
-
-    @pl.when(y == 1)
-    def _():
-        vout[...] = jnp.broadcast_to(apply_map(vin[0:1, :], whole, unit), (8, S))
-        chain(0, 3).start()
-        chain(1, 2).start()
-
-    @pl.when(y == 3)
-    def _():
-        carry.wait_recv()
-        vin[...] = jnp.broadcast_to(apply_map(vin[0:1, :], tin, unit), (8, S))
+        tell_state(1).wait_recv()
+
+    for owner in range(1, ny - 1):
+
+        @pl.when(y > owner)
+        def _():
+            tell_map(ny - 1, owner).wait_recv()
+            vin[...] = jnp.broadcast_to(apply_map(vin[0:1, :], tin[owner - 1], unit), (8, S))
 
     v = vin[0:1, :]
     za, zb, zc = lax.div(z, 4), lax.rem(lax.div(z, 2), 2), lax.rem(z, 2)
@@ -588,23 +589,21 @@
         for part in range(2):
             feat_copy(q, part, head).wait_send()
         head_copy(q, parts.at[peer(q)], landed.at[head], o_send, o_recv).wait_send()
-    for k in range(NZ // 2):
-        for d in range(2):
-            for c in range(len(CUTS)):
-                if goes(d, k, c):
-                    hop(d, k, c).wait_send()
-
-    @pl.when(y < 2)
+    for n in range(8):
+        for c in legs(n):
+            leg(n, c).wait_send()
+
+    @pl.when(y == 0)
     def _():
-        chain(0, 1).wait_send()
-
-    @pl.when(y == 1)
-    def _():
-        chain(1, 2).wait_send()
-
-    @pl.when(y == 2)
-    def _():
-        carry.wait_send()
+        for row in range(1, ny):
+            tell_state(row).wait_send()
+
+    for owner in range(1, ny - 1):
+
+        @pl.when(y == owner)
+        def _():
+            for row in range(owner + 1, ny):
+                tell_map(row, owner).wait_send()
 
     for ring in (ring_a1, ring_b1):
         ring.finish()
@@ -642,15 +641,15 @@
         pltpu.VMEM((4, MR, S), F32),
         pltpu.VMEM((NB, MR, S), F32),
         pltpu.VMEM((NZ + 1, MR, S), F32),
-        dma((2, NZ // 2, len(CUTS))),
-        dma((2, NZ // 2, len(CUTS))),
+        dma((len(LEGS), len(CUTS))),
+        dma((len(LEGS), len(CUTS))),
         pltpu.VMEM((4, MR, S), F32),
         pltpu.VMEM((8, S), F32),
         pltpu.VMEM((8, S), F32),
+        pltpu.VMEM((ny - 2, MR, S), F32),
         pltpu.VMEM((MR, S), F32),
-        pltpu.VMEM((MR, S), F32),
-        dma((3,)),
-        dma((2,)),
+        dma((ny,)),
+        dma((ny - 1,)),
         pltpu.VMEM((nhead, S, S), BF16),
         dma((2, nhead)),
         dma((2, nhead)),

time: 67.6 us -> 60.8 us (0.90)
  Pallas kernels: 66.8 us -> 60 us
    pallas_call x1, Pallas kernels: 66.1 us -> 59.3 us  [on_device(): pl.pallas_call(functools.partial(kernel, ntok, nhead), out_shape=tuple((p...]
where the time goes in v3:
time: 60.8 us; the launch traced here: 60.6 us
  Pallas kernels  60 us (99%)
  between operations  0.64 us (1%)
    pallas_call x1, Pallas kernels, on_device(): pl.pallas_call(functools.partial(kernel, ntok, nhead), out_shape=tuple((p...  59.3 us

profile of v3, /device:TPU:8, one launch (start us, length us, event | category | flops | bytes accessed | tf_op | source)
XLA Modules:
  0.0 60.6 jit_solution(1578567245915233597)
XLA Ops:
  0.6 59.3 %shard_map.128 = (f32[128,128]{1,0:T(8,128)S(1)}, bf16[128,128]{1,0:T(8,128)(2,1)S(1)}, bf16[128,128]{1,0:T(8,128)(2,1)S(1)}, f32[32,512]{1,0:T(8,128)S(1)}, f32[32,512]{1,0:T(8,128)S(1)}) custom-call(f32[128,128]{1,0:T(8,128)} %guess.1, f32[128,128]{1,0:T(8,128)} %drive.1, f32[128,128]{1,0:T(8,128)} %decay.1, f32[1,128]{1,0:T(1,128)} %bitcast.4, ...), custom_call_target="tpu_custom_call" | custom-call | tf_op jit(solution)/shard_map/pallas_call | solution.py:686
  59.9 0.7 %shard_map.129 = (f32[128,128]{1,0:T(8,128)}, bf16[128,128]{1,0:T(8,128)(2,1)}, bf16[128,128]{1,0:T(8,128)(2,1)}, f32[32,512]{1,0:T(8,128)}, f32[32,512]{1,0:T(8,128)}) custom-call(f32[128,128]{1,0:T(8,128)S(1)} %get-tuple-element.10.refs_0_, bf16[128,128]{1,0:T(8,128)(2,1)S(1)} %get-tuple-element.11.refs_1_, ...), custom_call_target="tpu_custom_call" | custom-call | tf_op jit(solution)/shard_map/pallas_call | solution.py:706

commit v4 on v3

--- a/solution.py
+++ b/solution.py
@@ -13,10 +13,9 @@
 NZ = 8
 NB, L = 8, 16
 MR = 144
-SENT = 136
-CUTS = ((0, 72), (72, 64))
-LEGS = ((2, 0), (-2, 0), (1, 0), (-1, 0), (1, -2), (-1, 2), (2, -2), (-2, 2))
-NEWTON = 14
+SPREAD = 86.0
+NEWTON = 11
+LEGS = (4, 3, 5, 2, 6, 1, 7)
 PIECES = 4
 ORDER = (4, 3, 6, 1, 5, 2, 7, 0)
 TURN = (2, 3, 1, 0)
@@ -66,6 +65,21 @@
 
 def dot_t(a, b):
     return lax.dot_general(a, b, (((1,), (1,)), ((), ())), preferred_element_type=F32)
+
+
+def encode(matrix, shift):
+    high, rest = split(shift)
+    low = (shift - high.astype(F32) - rest.astype(F32)).astype(BF16)
+    rows = [high[:1], rest[:1], low[:1], high[1:14]]
+    matrix = jnp.exp(jnp.clip(matrix, -1.01, 1.01) * SPREAD).astype(BF16)
+    return jnp.concatenate([matrix, jnp.concatenate([r.astype(F32) for r in rows], axis=0).astype(BF16)], axis=0)
+
+
+def decode(ref, at):
+    matrix = jnp.log(ref[at, 0:S, :].astype(F32)) * (1.0 / SPREAD)
+    tail = ref[at, S:MR, :].astype(F32)
+    shift = tail[0:1] + tail[1:2] + tail[2:3]
+    return jnp.concatenate([matrix, shift, jnp.zeros((MR - S - 1, S), F32)], axis=0)
 
 
 class Ring:
@@ -151,6 +165,7 @@
     w_down,
     w_sem,
     shifted,
+    behind,
     row_send,
     row_recv,
     wrot,
@@ -161,6 +176,7 @@
     bmaps,
     bpre,
     gath,
+    coded,
     gsend,
     grecv,
     table,
@@ -228,7 +244,7 @@
     after, before_me = lax.rem(tok + 1, ntok), lax.rem(tok + ntok - 1, ntok)
 
     barrier = pltpu.get_barrier_semaphore()
-    greet = [along_z(lax.rem(z + i, NZ)) for i in (1, 2, NZ - 1, NZ - 2)]
+    greet = [along_z(lax.rem(z + i, NZ)) for i in range(1, NZ)]
     greet += [along_y(lax.rem(y + i, ny)) for i in range(1, ny)]
     greet += [at_tok(after), at_tok(before_me)]
     greet += [at_head(peer(q)) for q in peers]
@@ -263,7 +279,7 @@
     pl.semaphore_wait(barrier, len(greet))
     row_copy = pltpu.make_async_remote_copy(
         src_ref=guess.at[pl.ds(S - 8, 8)],
-        dst_ref=shifted.at[pl.ds(0, 8)],
+        dst_ref=behind,
         send_sem=row_send,
         recv_sem=row_recv,
         device_id=at_tok(after),
@@ -295,16 +311,18 @@
     rot_t = 2.0 * v - unit
     wrot[...] = right(rot_t)
 
+    m = mixing[...]
+
+    def tangent(before, decay):
+        bent = jnp.tanh(before)
+        curve = 1.0 - bent * bent
+        return (1.0 - m) * decay + m * curve, m * (bent - curve * before)
+
     shifted[pl.ds(8, S), :] = guess[...]
-    row_copy.wait_recv()
-    before = shifted[pl.ds(7, S), :]
-    first = (lax.broadcasted_iota(jnp.int32, (S, S), 0) == 0) & (tok == 0)
-    before = jnp.where(first, init[...], before)
-    m = mixing[...]
-    bent = jnp.tanh(before)
-    curve = 1.0 - bent * bent
-    slopes[...] = (1.0 - m) * decay[...] + m * curve
-    offs[...] = product(left(m * (bent - curve * before)), wrot[...]) + drive[...]
+    first = lax.broadcasted_iota(jnp.int32, (S, S), 0) == 0
+    slope, push = tangent(jnp.where(first, 0.0, shifted[pl.ds(7, S), :]), decay[...])
+    slopes[...] = jnp.where(first, 1.0, slope)
+    offs[...] = product(left(jnp.where(first, 0.0, push)), wrot[...]) + drive[...]
 
     def advance(step, blocks, shift):
         rows = [left(blocks[b] * slopes[pl.ds(b * L + step, 1), :]) for b in range(NB)]
@@ -334,27 +352,26 @@
     bmaps[2] = compose(block_map(6), block_map(7))
     bpre[4] = compose(bpre[2], bmaps[0])
     bmaps[3] = compose(bmaps[1], bmaps[2])
-    gath[z] = compose(bpre[4], bmaps[3])
-
-    def leg(n, c, arriving=False):
-        way, owner = LEGS[n]
-        owner = owner - way if arriving else owner
-        part = gath.at[lax.rem(z + owner + 2 * NZ, NZ), pl.ds(*CUTS[c])]
+    own = compose(bpre[4], bmaps[3])
+    row_copy.wait_recv()
+    first_slope, first_push = tangent(jnp.where(tok == 0, init[...], behind[7:8, :]), decay[0:1, :])
+    own_shift = jnp.concatenate([apply_map(first_push, own, unit), jnp.zeros((MR - S - 1, S), F32)], axis=0)
+    own = column(first_slope, unit) * own[:S]
+    gath[z] = jnp.concatenate([own, own_shift], axis=0)
+    coded[z] = encode(own, own_shift)
+
+    def leg(r, owner):
         return pltpu.make_async_remote_copy(
-            src_ref=part,
-            dst_ref=part,
-            send_sem=gsend.at[n, c],
-            recv_sem=grecv.at[n, c],
-            device_id=along_z(lax.rem(z + way + NZ, NZ)),
+            src_ref=coded.at[owner],
+            dst_ref=coded.at[owner],
+            send_sem=gsend.at[r],
+            recv_sem=grecv.at[r],
+            device_id=along_z(lax.rem(z + r, NZ)),
             device_id_type=MESH,
         )
 
-    def legs(n):
-        return (n % 2,) if n >= 6 else (0, 1)
-
-    for n in range(4):
-        for c in legs(n):
-            leg(n, c).start()
+    for r in LEGS:
+        leg(r, z).start()
 
     for load in loads:
         load.wait()
@@ -367,12 +384,6 @@
             w_down[pl.ds(c * 2 * S, 2 * S), :],
             preferred_element_type=F32,
         )
-    for c in range(2):
-        for n in range(2):
-            leg(n, c, True).wait_recv()
-            if c in legs(6 + n):
-                leg(6 + n, c).start()
-            leg(4 + n, c).start()
     for h in range(nhead):
         ctrans[pl.ds(h * S, S), :] = cots[h].astype(F32).T.astype(BF16)
     bpre[3] = compose(bpre[2], block_map(2))
@@ -381,9 +392,10 @@
     bpre[7] = compose(bpre[6], block_map(6))
     gath[NZ] = none
     table[0] = none
-    for n in range(2, 8):
-        for c in legs(n):
-            leg(n, c, True).wait_recv()
+    for r in (1, 7, 2, 6, 3, 5, 4):
+        owner = lax.rem(z - r + NZ, NZ)
+        leg(r, owner).wait_recv()
+        gath[owner] = decode(coded, owner)
     pairs = [compose(gath[2 * i], gath[2 * i + 1]) for i in range(4)]
     table[1] = pairs[0]
     table[2] = pairs[2]
@@ -403,8 +415,8 @@
 
     def tell_map(row, owner):
         return pltpu.make_async_remote_copy(
-            src_ref=tout.at[pl.ds(0, SENT)],
-            dst_ref=tin.at[owner - 1, pl.ds(0, SENT)],
+            src_ref=tout,
+            dst_ref=tin.at[owner - 1],
             send_sem=v_send.at[row],
             recv_sem=v_recv.at[owner],
             device_id=along_y(row),
@@ -422,7 +434,7 @@
 
         @pl.when(y == owner)
         def _():
-            tout[...] = whole
+            tout[...] = encode(whole[:S], whole[S:])
             for row in range(ny - 1, owner, -1):
                 tell_map(row, owner).start()
 
@@ -435,14 +447,14 @@
         @pl.when(y > owner)
         def _():
             tell_map(ny - 1, owner).wait_recv()
-            vin[...] = jnp.broadcast_to(apply_map(vin[0:1, :], tin[owner - 1], unit), (8, S))
+            vin[...] = jnp.broadcast_to(apply_map(vin[0:1, :], decode(tin, owner - 1), unit), (8, S))
 
     v = vin[0:1, :]
     za, zb, zc = lax.div(z, 4), lax.rem(lax.div(z, 2), 2), lax.rem(z, 2)
     v = apply_map(v, table[3 * za], unit)
     v = apply_map(v, table[zb * (1 + za)], unit)
     v = apply_map(v, gath[zc * (z - 1) + (1 - zc) * NZ], unit)
-    enter = column(v, unit)
+    enter = column(v * first_slope + first_push, unit)
 
     half = S // 2
 
@@ -589,9 +601,8 @@
         for part in range(2):
             feat_copy(q, part, head).wait_send()
         head_copy(q, parts.at[peer(q)], landed.at[head], o_send, o_recv).wait_send()
-    for n in range(8):
-        for c in legs(n):
-            leg(n, c).wait_send()
+    for r in LEGS:
+        leg(r, z).wait_send()
 
     @pl.when(y == 0)
     def _():
@@ -631,6 +642,7 @@
         pltpu.VMEM((width, ff), BF16),
         dma((2,)),
         pltpu.VMEM((S + 8, S), F32),
+        pltpu.VMEM((8, S), F32),
         dma,
         dma,
         pltpu.VMEM((2 * S, 2 * S), BF16),
@@ -641,13 +653,14 @@
         pltpu.VMEM((4, MR, S), F32),
         pltpu.VMEM((NB, MR, S), F32),
         pltpu.VMEM((NZ + 1, MR, S), F32),
-        dma((len(LEGS), len(CUTS))),
-        dma((len(LEGS), len(CUTS))),
+        pltpu.VMEM((NZ, MR, S), BF16),
+        dma((NZ,)),
+        dma((NZ,)),
         pltpu.VMEM((4, MR, S), F32),
         pltpu.VMEM((8, S), F32),
         pltpu.VMEM((8, S), F32),
-        pltpu.VMEM((ny - 2, MR, S), F32),
-        pltpu.VMEM((MR, S), F32),
+        pltpu.VMEM((ny - 2, MR, S), BF16),
+        pltpu.VMEM((MR, S), BF16),
         dma((ny,)),
         dma((ny - 1,)),
         pltpu.VMEM((nhead, S, S), BF16),

time: 60.8 us -> 56.5 us (0.929)
  Pallas kernels: 60 us -> 55.8 us
    pallas_call x1, Pallas kernels: 59.3 us -> 55 us  [on_device(): pl.pallas_call(functools.partial(kernel, ntok, nhead), out_shape=tuple((p...]
where the time goes in v4:
time: 56.5 us; the launch traced here: 56.4 us
  Pallas kernels  55.8 us (99%)
  between operations  0.64 us (1%)
    pallas_call x1, Pallas kernels, on_device(): pl.pallas_call(functools.partial(kernel, ntok, nhead), out_shape=tuple((p...  55 us

profile of v4, /device:TPU:8, one launch (start us, length us, event | category | flops | bytes accessed | tf_op | source)
XLA Modules:
  0.0 56.4 jit_solution(18117462886981282889)
XLA Ops:
  0.6 55.0 %shard_map.128 = (f32[128,128]{1,0:T(8,128)S(1)}, bf16[128,128]{1,0:T(8,128)(2,1)S(1)}, bf16[128,128]{1,0:T(8,128)(2,1)S(1)}, f32[32,512]{1,0:T(8,128)S(1)}, f32[32,512]{1,0:T(8,128)S(1)}) custom-call(f32[128,128]{1,0:T(8,128)} %guess.1, f32[128,128]{1,0:T(8,128)} %drive.1, f32[128,128]{1,0:T(8,128)} %decay.1, f32[1,128]{1,0:T(1,128)} %bitcast.4, ...), custom_call_target="tpu_custom_call" | custom-call | tf_op jit(solution)/shard_map/pallas_call | solution.py:699
  55.7 0.7 %shard_map.129 = (f32[128,128]{1,0:T(8,128)}, bf16[128,128]{1,0:T(8,128)(2,1)}, bf16[128,128]{1,0:T(8,128)(2,1)}, f32[32,512]{1,0:T(8,128)}, f32[32,512]{1,0:T(8,128)}) custom-call(f32[128,128]{1,0:T(8,128)S(1)} %get-tuple-element.10.refs_0_, bf16[128,128]{1,0:T(8,128)(2,1)S(1)} %get-tuple-element.11.refs_1_, ...), custom_call_target="tpu_custom_call" | custom-call | tf_op jit(solution)/shard_map/pallas_call | solution.py:719

commit v5 on v4

--- a/solution.py
+++ b/solution.py
@@ -273,8 +273,12 @@
         return out[S:], out[:S], square / (2.0 - square)
 
     v, t = (unit - k) * scale, (unit - kk) * scale
-    for _ in range(NEWTON // 2):
+    for _ in range(NEWTON):
         v, t, gap = newton(v, t, gap)
+    t = jnp.dot(a, v, precision=lax.Precision.HIGHEST, preferred_element_type=F32)
+    v = v + mm(v, unit - t)
+    rot_t = 2.0 * v - unit
+    wrot[...] = right(rot_t)
 
     pl.semaphore_wait(barrier, len(greet))
     row_copy = pltpu.make_async_remote_copy(
@@ -303,13 +307,6 @@
     for q in peers:
         head_copy(q, cot, cots.at[head], c_send, c_recv).start()
     cots[head] = cot[...]
-
-    for _ in range(NEWTON - NEWTON // 2):
-        v, t, gap = newton(v, t, gap)
-    t = jnp.dot(a, v, precision=lax.Precision.HIGHEST, preferred_element_type=F32)
-    v = v + mm(v, unit - t)
-    rot_t = 2.0 * v - unit
-    wrot[...] = right(rot_t)
 
     m = mixing[...]
 
@@ -570,11 +567,17 @@
             down_copy(r).start()
 
     ring_b1.advance(0, False)
+    ring_b1.advance(1, True)
     ring_a1.advance(0, False)
-    ring_b1.advance(1, True)
     ring_b1.advance(1, False)
     ring_b1.advance(2, True)
     ring_b1.advance(2, False)
+    up_part(0)
+    up_part(2)
+    up_part(1)
+    up_part(3)
+    for c in (0, 2, 1, 3):
+        down_part(c)
     for q in peers:
         head_copy(q, parts.at[peer(q)], landed.at[back(q)], o_send, o_recv).wait_recv()
     outs = [parts[head, i].astype(F32) for i in range(2)]
@@ -582,12 +585,6 @@
         outs = [outs[i] + landed[back(q), i].astype(F32) for i in range(2)]
     mlp_out[...] = outs[0].astype(BF16)
     sgrad_out[...] = outs[1].astype(BF16)
-    up_part(0)
-    up_part(2)
-    up_part(1)
-    up_part(3)
-    for c in (0, 2, 1, 3):
-        down_part(c)
     for r in (1, 7, 2, 6, 3, 5, 4):
         up_copy(r).wait_recv()
         gup_out[...] += la2[r].astype(F32)

time: 56.5 us -> 54.3 us (0.961)
  Pallas kernels: 55.8 us -> 53.5 us
    pallas_call x1, Pallas kernels: 55 us -> 52.8 us  [on_device(): pl.pallas_call(functools.partial(kernel, ntok, nhead), out_shape=tuple((p...]
where the time goes in v5:
time: 54.3 us; the launch traced here: 54.1 us
  Pallas kernels  53.5 us (99%)
  between operations  0.64 us (1%)
    pallas_call x1, Pallas kernels, on_device(): pl.pallas_call(functools.partial(kernel, ntok, nhead), out_shape=tuple((p...  52.8 us

profile of v5, /device:TPU:8, one launch (start us, length us, event | category | flops | bytes accessed | tf_op | source)
XLA Modules:
  0.0 54.1 jit_solution(16845976679158809723)
XLA Ops:
  0.6 52.8 %shard_map.128 = (f32[128,128]{1,0:T(8,128)S(1)}, bf16[128,128]{1,0:T(8,128)(2,1)S(1)}, bf16[128,128]{1,0:T(8,128)(2,1)S(1)}, f32[32,512]{1,0:T(8,128)S(1)}, f32[32,512]{1,0:T(8,128)S(1)}) custom-call(f32[128,128]{1,0:T(8,128)} %guess.1, f32[128,128]{1,0:T(8,128)} %drive.1, f32[128,128]{1,0:T(8,128)} %decay.1, f32[1,128]{1,0:T(1,128)} %bitcast.4, ...), custom_call_target="tpu_custom_call" | custom-call | tf_op jit(solution)/shard_map/pallas_call | solution.py:696
  53.4 0.7 %shard_map.129 = (f32[128,128]{1,0:T(8,128)}, bf16[128,128]{1,0:T(8,128)(2,1)}, bf16[128,128]{1,0:T(8,128)(2,1)}, f32[32,512]{1,0:T(8,128)}, f32[32,512]{1,0:T(8,128)}) custom-call(f32[128,128]{1,0:T(8,128)S(1)} %get-tuple-element.10.refs_0_, bf16[128,128]{1,0:T(8,128)(2,1)S(1)} %get-tuple-element.11.refs_1_, ...), custom_call_target="tpu_custom_call" | custom-call | tf_op jit(solution)/shard_map/pallas_call | solution.py:716

commit v6 on v5

--- a/solution.py
+++ b/solution.py
@@ -168,6 +168,7 @@
     behind,
     row_send,
     row_recv,
+    rot,
     wrot,
     slopes,
     offs,
@@ -278,6 +279,7 @@
     t = jnp.dot(a, v, precision=lax.Precision.HIGHEST, preferred_element_type=F32)
     v = v + mm(v, unit - t)
     rot_t = 2.0 * v - unit
+    rot[...] = rot_t
     wrot[...] = right(rot_t)
 
     pl.semaphore_wait(barrier, len(greet))
@@ -330,7 +332,10 @@
             pre_maps[b * L + step] = out[b * S : (b + 1) * S]
         shifts[step] = out[NB * S : NB * S + NB] + offs[pl.ds(step, NB, stride=L), :]
 
-    advance(0, [unit] * NB, jnp.zeros((NB, S), F32))
+    pre_maps[0] = rot[...]
+    for b in range(1, NB):
+        pre_maps[b * L] = column(slopes[b * L : b * L + 1, :], unit) * rot[...]
+    shifts[0] = offs[pl.ds(0, NB, stride=L), :]
 
     for step in range(1, L):
         advance(step, [pre_maps[b * L + step - 1] for b in range(NB)], shifts[step - 1])
@@ -389,7 +394,7 @@
     bpre[7] = compose(bpre[6], block_map(6))
     gath[NZ] = none
     table[0] = none
-    for r in (1, 7, 2, 6, 3, 5, 4):
+    for r in LEGS:
         owner = lax.rem(z - r + NZ, NZ)
         leg(r, owner).wait_recv()
         gath[owner] = decode(coded, owner)
@@ -476,7 +481,7 @@
         states_out[b * L : (b + 1) * L, :] = out
         feats[head, b * L : (b + 1) * L, :] = out.astype(BF16)
         if b % (NB // 2) == NB // 2 - 1:
-            for q in peers:
+            for q in peers[-2:] + peers[1:-2] + peers[:1]:
                 feat_copy(q, b // (NB // 2), head).start()
 
     def of_chip(dx, rows):
@@ -642,6 +647,7 @@
         pltpu.VMEM((8, S), F32),
         dma,
         dma,
+        pltpu.VMEM((S, S), F32),
         pltpu.VMEM((2 * S, 2 * S), BF16),
         pltpu.VMEM((S, S), F32),
         pltpu.VMEM((S, S), F32),

time: 54.3 us -> 53.9 us (level)
  no operation moved by 1% of the time
where the time goes in v6:
time: 53.9 us; the launch traced here: 53.8 us
  Pallas kernels  53.1 us (99%)
  between operations  0.64 us (1%)
    pallas_call x1, Pallas kernels, on_device(): pl.pallas_call(functools.partial(kernel, ntok, nhead), out_shape=tuple((p...  52.4 us

profile of v6, /device:TPU:8, one launch (start us, length us, event | category | flops | bytes accessed | tf_op | source)
XLA Modules:
  0.0 53.8 jit_solution(3272447120881068602)
XLA Ops:
  0.6 52.4 %shard_map.128 = (f32[128,128]{1,0:T(8,128)S(1)}, bf16[128,128]{1,0:T(8,128)(2,1)S(1)}, bf16[128,128]{1,0:T(8,128)(2,1)S(1)}, f32[32,512]{1,0:T(8,128)S(1)}, f32[32,512]{1,0:T(8,128)S(1)}) custom-call(f32[128,128]{1,0:T(8,128)} %guess.1, f32[128,128]{1,0:T(8,128)} %drive.1, f32[128,128]{1,0:T(8,128)} %decay.1, f32[1,128]{1,0:T(1,128)} %bitcast.4, ...), custom_call_target="tpu_custom_call" | custom-call | tf_op jit(solution)/shard_map/pallas_call | solution.py:702
  53.1 0.7 %shard_map.129 = (f32[128,128]{1,0:T(8,128)}, bf16[128,128]{1,0:T(8,128)(2,1)}, bf16[128,128]{1,0:T(8,128)(2,1)}, f32[32,512]{1,0:T(8,128)}, f32[32,512]{1,0:T(8,128)}) custom-call(f32[128,128]{1,0:T(8,128)S(1)} %get-tuple-element.10.refs_0_, bf16[128,128]{1,0:T(8,128)(2,1)S(1)} %get-tuple-element.11.refs_1_, ...), custom_call_target="tpu_custom_call" | custom-call | tf_op jit(solution)/shard_map/pallas_call | solution.py:722
